TPU v7x, 256 devices: a whole 4x4x8 slice. The times are simulated.
256 devices in a mesh: band: 4 (over y_lo, core), grid: 64 (over z, x, y_hi).
Axes of the slice: x: 4, y: 4 (y_hi: 2, y_lo: 2; y = y_hi * 2 + y_lo), z: 8, core: 2. Of those that a mesh axis runs over, the one named last changes fastest.
Arguments:
- orbitals: float32 [128, 64, 128, 128], P('band', 'grid'), may hold values from -8 to 8
- trials: float32 [4, 64, 128, 128], P('band', 'grid'), may hold values from -6 to 6
- owner_group: int32 [4], replicated, may hold values from 0 to 3, as said below
- block_index: int32 [4], replicated, may hold values from 0 to 3, as said below
Outputs:
- exchange_applied: float32 [4, 64, 128, 128], P('band', 'grid')
Inputs may be any that keep to these rules, and one draw needn't show every extreme that they name: `owner_group`: no two steps name the same band group. `block_index`: no two steps name the same block.
All inputs are finite; a program needn't handle non-finite values.
Results may differ from a plain program's by a relative error of at most 0.0001.
Values sent between devices are 32-bit elements; how exact they have to be, the bound alone decides.
No kernel may reach another device: no remote copies, remote signals or barrier semaphores. Data moves between devices by JAX's collectives and lax.ppermute only.
A program may use at most 64 MiB of HBM per device.

v0:
```python
import math

import jax
import jax.numpy as jnp
import ml_dtypes
import numpy as np
from jax import lax
from jax.experimental import pallas as pl
from jax.experimental.pallas import tpu as pltpu
from jax.sharding import Mesh, PartitionSpec as P

BLOCK = 8
NX, NY, NZ = 64, 128, 128
AXES = ("yl", "c", "zh", "z0", "x", "yh")
SIZES = (2, 2, 4, 2, 4, 2)
SPREAD = ("z0", "x", "yh")
FAR = 4
SHARE = 16
ROWS = NY // SHARE
KEEP = BLOCK // FAR
VMEM = 48 << 20


def frequencies(length):
    index = np.arange(length)
    return np.where(index <= length // 2, index, index - length // 2)


def basis(length):
    index = np.arange(length)
    freq = frequencies(length)
    angle = 2.0 * np.pi / length * (freq[:, None] * index[None, :] % length)
    rows = np.where((index <= length // 2)[:, None], np.cos(angle), np.sin(angle))
    scale = np.where((index == 0) | (index == length // 2), 1.0, 2.0) / length
    return rows * np.sqrt(scale)[:, None]


def halves(table):
    high = table.astype(np.float32).astype(ml_dtypes.bfloat16)
    low = (table - high.astype(np.float64)).astype(ml_dtypes.bfloat16)
    return high, low


def right_table(table):
    high, low = halves(table)
    return np.concatenate(
        [np.concatenate([high, low], 1), np.concatenate([high, np.zeros_like(low)], 1)], 0
    )


def left_table(table):
    high, low = halves(table)
    return np.concatenate([high, high, low], 1)


def split(value):
    high = value.astype(jnp.bfloat16)
    low = (value - high.astype(jnp.float32)).astype(jnp.bfloat16)
    return high, low


def times_right(value, table):
    high, low = split(value)
    both = jnp.dot(
        jnp.concatenate([high, low], axis=1), table, preferred_element_type=jnp.float32
    )
    size = both.shape[1] // 2
    return both[:, :size] + both[:, size:]


def times_left(table, value):
    high, low = split(value)
    return jnp.dot(
        table, jnp.concatenate([high, low, high], axis=0), preferred_element_type=jnp.float32
    )


def forward_kernel(trial, own, second, third, fourth, right, left, out):
    for plane in range(trial.shape[0]):
        for slot, bands in enumerate((own, second, third, fourth)):
            pair = jnp.concatenate(
                [trial[plane] * bands[plane, 0], trial[plane] * bands[plane, 1]], axis=0
            )
            pair = times_right(pair, right[...])
            pair = jnp.concatenate([pair[:NY], pair[NY:]], axis=1)
            pair = times_left(left[...], pair)
            for k in range(KEEP):
                out[:, slot * KEEP + k, plane] = pair[:, k * NZ : (k + 1) * NZ].reshape(
                    SHARE, ROWS, NZ
                )


def inverse_kernel(potential, own, second, third, fourth, right, left, out):
    for plane in range(out.shape[0]):
        total = jnp.zeros((NY, NZ), jnp.float32)
        for slot, bands in enumerate((own, second, third, fourth)):
            pair = jnp.concatenate(
                [potential[:, slot * KEEP + k, plane].reshape(NY, NZ) for k in range(KEEP)],
                axis=1,
            )
            pair = times_left(left[...], pair)
            pair = jnp.concatenate([pair[:, :NZ], pair[:, NZ:]], axis=0)
            pair = times_right(pair, right[...])
            total = total + pair[:NY] * bands[plane, 0] + pair[NY:] * bands[plane, 1]
        out[plane] = total * (-math.sqrt(NX * NY * NZ) / BLOCK)


def solve_kernel(near, rest, squares, base, ahead, back, near_out, rest_out):
    bands = near.shape[1]
    for row in range(ROWS):
        kernel = 1.0 / (squares[...] + base[row : row + 1, :])
        kernel = jnp.concatenate([kernel, kernel], axis=1)
        for band in range(0, bands, 2):
            columns = jnp.concatenate(
                [
                    jnp.concatenate(
                        [near[:, b, 0, row, :]]
                        + [rest[:, b, p, row, :] for p in range(FAR - 1)],
                        axis=0,
                    )
                    for b in (band, band + 1)
                ],
                axis=1,
            )
            columns = times_left(ahead[...], columns) * kernel
            columns = times_left(back[...], columns)
            for i in range(2):
                part = columns[:, i * NZ : (i + 1) * NZ]
                near_out[:, band + i, 0, row, :] = part[:SHARE]
                for p in range(FAR - 1):
                    rest_out[:, band + i, p, row, :] = part[(p + 1) * SHARE : (p + 2) * SHARE]


def params():
    return pltpu.CompilerParams(vmem_limit_bytes=VMEM)


def specs(count):
    return [pl.BlockSpec(memory_space=pltpu.VMEM)] * count


def forward(trial, bands, right, left):
    planes = trial.shape[0]
    shape = (SHARE, 4 * KEEP, planes, ROWS, NZ)
    return pl.pallas_call(
        forward_kernel,
        out_shape=jax.ShapeDtypeStruct(shape, jnp.float32),
        in_specs=specs(7),
        out_specs=specs(1)[0],
        compiler_params=params(),
        cost_estimate=pl.CostEstimate(
            flops=planes * 8 * 128 * 128 * 256 * 6, bytes_accessed=planes << 20, transcendentals=0
        ),
        name="forward_planes",
    )(trial, *bands, right, left)


def inverse(potential, bands, right, left):
    planes = potential.shape[2]
    return pl.pallas_call(
        inverse_kernel,
        out_shape=jax.ShapeDtypeStruct((planes, NY, NZ), jnp.float32),
        in_specs=specs(7),
        out_specs=specs(1)[0],
        compiler_params=params(),
        cost_estimate=pl.CostEstimate(
            flops=planes * 8 * 128 * 128 * 256 * 6, bytes_accessed=planes << 20, transcendentals=0
        ),
        name="inverse_planes",
    )(potential, *bands, right, left)


def solve(near, rest, squares, base, ahead, back):
    return pl.pallas_call(
        solve_kernel,
        out_shape=(
            jax.ShapeDtypeStruct(near.shape, jnp.float32),
            jax.ShapeDtypeStruct(rest.shape, jnp.float32),
        ),
        in_specs=specs(6),
        out_specs=tuple(specs(2)),
        compiler_params=params(),
        cost_estimate=pl.CostEstimate(
            flops=8 * 64 * 64 * 1024 * 12, bytes_accessed=4 << 20, transcendentals=0
        ),
        name="solve_columns",
    )(near, rest, squares, base, ahead, back)


def exchange(value):
    return lax.all_to_all(value, SPREAD, 0, 0, tiled=True)


def swap(value, axis):
    return lax.ppermute(value, axis, [(0, 1), (1, 0)])


def all_blocks(own):
    across = swap(own, "yl")
    return own, swap(own, "c"), across, swap(across, "c")


def local(orbitals, trials, owner_group, block_index):
    plane_table = basis(NY)
    column_table = basis(NX)
    right_ahead = jnp.asarray(right_table(plane_table.T))
    left_ahead = jnp.asarray(left_table(plane_table))
    right_back = jnp.asarray(right_table(plane_table))
    left_back = jnp.asarray(left_table(plane_table.T))
    column_ahead = jnp.asarray(left_table(column_table))
    column_back = jnp.asarray(left_table(column_table.T))
    squares = np.broadcast_to((frequencies(NX)[:, None] ** 2), (NX, NZ)).astype(np.float32)
    grid_squares = 1 + frequencies(NY)[:, None] ** 2 + frequencies(NZ)[None, :] ** 2
    base = lax.dynamic_slice_in_dim(
        jnp.asarray(grid_squares.astype(np.float32)), lax.axis_index(SPREAD) * ROWS, ROWS, 0
    )

    group = lax.axis_index(("yl", "c"))
    mine = jnp.sum(jnp.where(owner_group == group, block_index, 0)) * BLOCK
    far = lax.axis_index("zh")

    def bands_for(place):
        start = mine + lax.rem(place + FAR, FAR) * KEEP
        return lax.dynamic_slice_in_dim(orbitals[:, 0], start, KEEP, 0)

    trial = trials[0]
    near_bands = all_blocks(bands_for(far)[None])
    arrived = []
    for step in range(1, FAR):
        packet = jnp.concatenate([bands_for(far - step), trial], axis=0)
        perm = [(i, (i - step) % FAR) for i in range(FAR)]
        arrived.append(lax.ppermute(packet, "zh", perm))
    near = exchange(forward(trial, near_bands, right_ahead, left_ahead))

    rest_bands = all_blocks(jnp.stack([packet[:KEEP] for packet in arrived]))
    rest_trial = jnp.stack([packet[KEEP] for packet in arrived])
    rest = exchange(forward(rest_trial, rest_bands, right_ahead, left_ahead))

    near, rest = solve(
        near, rest, jnp.asarray(squares), base, column_ahead, column_back
    )
    rest = inverse(exchange(rest), rest_bands, right_back, left_back)
    returned = []
    for step in range(1, FAR):
        perm = [(i, (i + step) % FAR) for i in range(FAR)]
        returned.append(lax.ppermute(rest[step - 1], "zh", perm))
    near = inverse(exchange(near), near_bands, right_back, left_back)
    return (near[0] + returned[0] + returned[1] + returned[2])[None, None]


def solution(mesh):
    fine = Mesh(mesh.devices.reshape(SIZES), AXES)
    spec = P(("yl", "c"), ("zh", "z0", "x", "yh"), None, None)
    return jax.shard_map(
        local,
        mesh=fine,
        in_specs=(spec, spec, P(), P()),
        out_specs=spec,
        check_vma=False,
    )
```

profile of v0, /device:TPU:2, one launch (start us, length us, event | category | flops | bytes accessed | tf_op | source)
XLA Modules:
  0.0 147.3 jit_solution(12917845729852440156)
XLA Ops:
  0.0 0.0 copy-start.13
  0.0 0.0 copy-start.3
  0.0 1.4 fusion.3
  2.1 1.1 dynamic-slice_bitcast_fusion.2
  3.2 0.9 pad_maximum_fusion.3
  4.1 6.4 %collective-permute-start.3 = (f32[3,128,128]{2,1,0:T(8,128)S(1)}, f32[3,128,128]{2,1,0:T(8,128)S(1)}, u32[]{:S(2)}, u32[]{:S(2)}) collective-permute-start(f32[3,128,128]{2,1,0:T(8,128)S(1)} %get-tuple-element.16), channel_id=1, source_target_pairs={{0,48},{16,0},{32,16},{48,32},{1,49},{17,1},{33,17},{49,33},{2,50}... | collective-permute-start | bytes 589832 | tf_op jit(solution)/shard_map/ppermute | solution.py:232
  10.5 1.6 %collective-permute-start.1 = (f32[1,2,128,128]{3,2,1,0:T(8,128)S(1)}, f32[1,2,128,128]{3,2,1,0:T(8,128)S(1)}, u32[]{:S(2)}, u32[]{:S(2)}) collective-permute-start(f32[1,2,128,128]{3,2,1,0:T(8,128)S(1)} %get-tuple-element.10.own), channel_id=1, source_target_pairs={{0,128},{128,0},{1,129},{129,1},{2,130},{130,2},{3,131},{131,3},{4... | collective-permute-start | bytes 393224 | tf_op jit(solution)/shard_map/ppermute | solution.py:195
  12.1 0.0 collective-permute-start
  12.1 1.0 collective-permute-start.4
  13.0 2.8 %collective-permute-start.5 = (f32[3,128,128]{2,1,0:T(8,128)S(1)}, f32[3,128,128]{2,1,0:T(8,128)S(1)}, u32[]{:S(2)}, u32[]{:S(2)}) collective-permute-start(f32[3,128,128]{2,1,0:T(8,128)S(1)} %get-tuple-element.18), channel_id=1, source_target_pairs={{0,16},{16,32},{32,48},{48,0},{1,17},{17,33},{33,49},{49,1},{2,18}... | collective-permute-start | bytes 589832 | tf_op jit(solution)/shard_map/ppermute | solution.py:232
  15.9 0.0 collective-permute-done.1.third
  15.9 0.0 collective-permute-start.2
  15.9 11.4 %collective-permute-done.3 = f32[3,128,128]{2,1,0:T(8,128)S(1)} collective-permute-done((f32[3,128,128]{2,1,0:T(8,128)S(1)}, f32[3,128,128]{2,1,0:T(8,128)S(1)}, u32[]{:S(2)}, u32[]{:S(2)}) %collective-permute-start.3) | collective-permute-done | bytes 196640 | tf_op jit(solution)/shard_map/ppermute | solution.py:232
  27.3 0.8 collective-permute-done.4
  28.1 0.0 collective-permute-done.second
  28.2 0.0 collective-permute-done.2.fourth
  28.2 0.0 copy-done.5
  28.2 0.0 copy-done.13
  28.2 0.0 copy-done.3
  28.2 0.0 copy-done.14
  28.2 1.4 forward_planes.2
  29.6 0.6 copy-done.7
  30.3 0.6 copy-done.9
  30.9 9.2 %all-to-all-start = ((f32[16,8,1,8,128]{4,3,2,1,0:T(8,128)}), f32[16,8,1,8,128]{4,3,2,1,0:T(8,128)S(1)}, u32[]{:S(2)}, u32[]{:S(2)}) async-start(f32[16,8,1,8,128]{4,3,2,1,0:T(8,128)} %forward_planes.2), calls=%async_computation | async-start | bytes 1048576 | tf_op jit(solution)/shard_map/all_to_all | solution.py:191
  40.2 0.0 collective-permute-done.5
  40.2 0.5 collective-permute-start.7
  40.8 0.0 collective-permute-start.6
  40.8 14.8 %collective-permute-done.7.third = f32[3,2,128,128]{3,2,1,0:T(8,128)S(1)} collective-permute-done((f32[3,2,128,128]{3,2,1,0:T(8,128)S(1)}, f32[3,2,128,128]{3,2,1,0:T(8,128)S(1)}, u32[]{:S(2)}, u32[]{:S(2)}) %collective-permute-start.7) | collective-permute-done | bytes 393248 | tf_op jit(solution)/shard_map/ppermute | solution.py:195
  55.6 0.0 collective-permute-start.8
  55.7 0.0 collective-permute-done.6.second
  55.7 1.6 %collective-permute-done.8.fourth = f32[3,2,128,128]{3,2,1,0:T(8,128)S(1)} collective-permute-done((f32[3,2,128,128]{3,2,1,0:T(8,128)S(1)}, f32[3,2,128,128]{3,2,1,0:T(8,128)S(1)}, u32[]{:S(2)}, u32[]{:S(2)}) %collective-permute-start.8) | collective-permute-done | bytes 393248 | tf_op jit(solution)/shard_map/ppermute | solution.py:195
  57.3 2.4 %forward_planes.3 = f32[16,8,3,8,128]{4,3,2,1,0:T(8,128)} custom-call(f32[3,128,128]{2,1,0:T(8,128)S(1)} %pad_maximum_fusion.4.trial, f32[3,2,128,128]{3,2,1,0:T(8,128)S(1)} %pad_maximum_fusion.own, f32[3,2,128,128]{3,2,1,0:T(8,128)S(1)} %collective-permute-done.6.second, f32[3,2,128,128]{3,2,1,0:T(8,128)S(1)} %collective-permute-done.7.third, ...), custom_call_target="tpu_custom_call" | custom-call | flops 603979776 | bytes 3145728 | tf_op jit(solution)/shard_map/forward_planes/pallas_call | solution.py:145
  59.7 0.8 copy-done
  60.5 0.0 all-to-all-done.near
  60.5 8.3 %all-to-all-start.1 = ((f32[16,8,3,8,128]{4,3,2,1,0:T(8,128)}), f32[16,8,3,8,128]{4,3,2,1,0:T(8,128)S(1)}, u32[]{:S(2)}, u32[]{:S(2)}) async-start(f32[16,8,3,8,128]{4,3,2,1,0:T(8,128)} %forward_planes.3), calls=%async_computation.1 | async-start | bytes 3145728 | tf_op jit(solution)/shard_map/all_to_all | solution.py:191
  68.8 0.7 constant_dynamic-slice_fusion.base
  69.5 24.6 %all-to-all-done.1.rest = f32[16,8,3,8,128]{4,3,2,1,0:T(8,128)S(1)} async-done(((f32[16,8,3,8,128]{4,3,2,1,0:T(8,128)}), f32[16,8,3,8,128]{4,3,2,1,0:T(8,128)S(1)}, u32[]{:S(2)}, u32[]{:S(2)}) %all-to-all-start.1) | async-done | bytes 1572896 | tf_op jit(solution)/shard_map/all_to_all | solution.py:191
  94.1 0.0 copy-done.15
  94.1 0.0 copy-done.16
  94.1 0.0 copy-done.17
  94.1 3.1 %solve_columns.1 = (f32[16,8,1,8,128]{4,3,2,1,0:T(8,128)S(1)}, f32[16,8,3,8,128]{4,3,2,1,0:T(8,128)S(1)}) custom-call(f32[16,8,1,8,128]{4,3,2,1,0:T(8,128)S(1)} %all-to-all-done.near, f32[16,8,3,8,128]{4,3,2,1,0:T(8,128)S(1)} %all-to-all-done.1.rest, f32[64,128]{1,0:T(8,128)S(1)} %copy-done.15, f32[8,128]{1,0:T(8,128)S(1)} %constant_dynamic-slice_fusion.base, ...), custom_call_target="tpu_custom_call" | custom-call | flops 402653184 | bytes 4194304 | tf_op jit(solution)/shard_map/solve_columns/pallas_call | solution.py:174
  97.3 0.0 copy-start.4
  97.3 0.0 copy-start.2
  97.3 28.0 %all_to_all.20.potential = f32[16,8,3,8,128]{4,3,2,1,0:T(8,128)S(1)} all-to-all(f32[16,8,3,8,128]{4,3,2,1,0:T(8,128)S(1)} %get-tuple-element.8), channel_id=1, replica_groups=mesh['yl'=2,'c'=2,'zh'=4,'z0'=2,'x'=4,'yh'=2] {'z0','x','yh'}, dimensions={0} | all-to-all | bytes 3145728 | tf_op jit(solution)/shard_map/all_to_all | solution.py:191
  125.3 0.0 copy-done.4
  125.3 5.3 %all-to-all-start.2 = ((f32[16,8,1,8,128]{4,3,2,1,0:T(8,128)}), f32[16,8,1,8,128]{4,3,2,1,0:T(8,128)S(1)}, u32[]{:S(2)}, u32[]{:S(2)}) async-start(f32[16,8,1,8,128]{4,3,2,1,0:T(8,128)} %copy-done.4), calls=%async_computation.2 | async-start | bytes 1048576 | tf_op jit(solution)/shard_map/all_to_all | solution.py:191
  130.6 0.0 copy-done.2
  130.6 0.0 copy-start.1
  130.6 1.0 copy-done.1
  131.6 0.9 copy-done.11
  132.5 1.1 inverse_planes.3
  133.6 0.1 collective-permute-start.9
  133.7 4.1 %collective-permute-start.11 = (f32[128,128]{1,0:T(8,128)S(1)}, f32[128,128]{1,0:T(8,128)S(1)}, u32[]{:S(2)}, u32[]{:S(2)}) collective-permute-start(f32[128,128]{1,0:T(8,128)S(1)} %get-tuple-element.14), channel_id=1, source_target_pairs={{0,48},{16,0},{32,16},{48,32},{1,49},{17,1},{33,17},{49,33},{2,50}... | collective-permute-start | bytes 196616 | tf_op jit(solution)/shard_map/ppermute | solution.py:246
  137.9 2.8 %collective-permute-start.10 = (f32[128,128]{1,0:T(8,128)S(1)}, f32[128,128]{1,0:T(8,128)S(1)}, u32[]{:S(2)}, u32[]{:S(2)}) collective-permute-start(f32[128,128]{1,0:T(8,128)S(1)} %get-tuple-element.15), channel_id=1, source_target_pairs={{0,32},{16,48},{32,0},{48,16},{1,33},{17,49},{33,1},{49,17},{2,34}... | collective-permute-start | bytes 196616 | tf_op jit(solution)/shard_map/ppermute | solution.py:246
  140.7 0.0 all-to-all-done.2.potential
  140.7 0.9 copy-done.6
  141.6 0.9 copy-done.8
  142.5 0.9 copy-done.10
  143.4 0.9 copy-done.12
  144.3 0.6 inverse_planes.2
  144.9 0.0 collective-permute-done.9
  144.9 0.0 collective-permute-done.11
  144.9 1.8 %collective-permute-done.10 = f32[128,128]{1,0:T(8,128)S(1)} collective-permute-done((f32[128,128]{1,0:T(8,128)S(1)}, f32[128,128]{1,0:T(8,128)S(1)}, u32[]{:S(2)}, u32[]{:S(2)}) %collective-permute-start.10) | collective-permute-done | bytes 65568 | tf_op jit(solution)/shard_map/ppermute | solution.py:246
  146.7 0.6 fusion.2
  (22 shorter events, 0.1 us)
Async XLA Ops:
  0.0 28.2 %copy-start.13 = (bf16[128,384]{1,0:T(8,128)(2,1)S(1)}, bf16[128,384]{1,0:T(8,128)(2,1)}, u32[]{:S(2)}) copy-start(bf16[128,384]{1,0:T(8,128)(2,1)} %constant.74.clone.left) | copy-start | bytes 294916
  0.0 28.2 %copy-start.3 = (bf16[256,256]{1,0:T(8,128)(2,1)S(1)}, bf16[256,256]{1,0:T(8,128)(2,1)}, u32[]{:S(2)}) copy-start(bf16[256,256]{1,0:T(8,128)(2,1)} %constant.73.clone.right) | copy-start | bytes 393220
  0.0 28.2 %copy-start.14 = (f32[1,1,128,128]{3,2,1,0:T(8,128)S(1)}, f32[1,1,128,128]{3,2,1,0:T(8,128)}, u32[]{:S(2)}) copy-start(f32[1,1,128,128]{3,2,1,0:T(8,128)} %param.13) | copy-start | bytes 196612
  4.1 23.2 %collective-permute-start.3 = (f32[3,128,128]{2,1,0:T(8,128)S(1)}, f32[3,128,128]{2,1,0:T(8,128)S(1)}, u32[]{:S(2)}, u32[]{:S(2)}) collective-permute-start(f32[3,128,128]{2,1,0:T(8,128)S(1)} %get-tuple-element.16), channel_id=1, source_target_pairs={{0,48},{16,0},{32,16},{48,32},{1,49},{17,1},{33,17},{49,33},{2,50}... | collective-permute-start | bytes 589832 | tf_op jit(solution)/shard_map/ppermute | solution.py:232
  10.5 5.4 %collective-permute-start.1 = (f32[1,2,128,128]{3,2,1,0:T(8,128)S(1)}, f32[1,2,128,128]{3,2,1,0:T(8,128)S(1)}, u32[]{:S(2)}, u32[]{:S(2)}) collective-permute-start(f32[1,2,128,128]{3,2,1,0:T(8,128)S(1)} %get-tuple-element.10.own), channel_id=1, source_target_pairs={{0,128},{128,0},{1,129},{129,1},{2,130},{130,2},{3,131},{131,3},{4... | collective-permute-start | bytes 393224 | tf_op jit(solution)/shard_map/ppermute | solution.py:195
  12.1 16.1 %collective-permute-start = (f32[1,2,128,128]{3,2,1,0:T(8,128)S(1)}, f32[1,2,128,128]{3,2,1,0:T(8,128)S(1)}, u32[]{:S(2)}, u32[]{:S(2)}) collective-permute-start(f32[1,2,128,128]{3,2,1,0:T(8,128)S(1)} %get-tuple-element.10.own), channel_id=1, source_target_pairs={{0,64},{64,0},{1,65},{65,1},{2,66},{66,2},{3,67},{67,3},{4,68},{68... | collective-permute-start | bytes 393224 | tf_op jit(solution)/shard_map/ppermute | solution.py:195
  12.1 16.1 %collective-permute-start.4 = (f32[3,128,128]{2,1,0:T(8,128)S(1)}, f32[3,128,128]{2,1,0:T(8,128)S(1)}, u32[]{:S(2)}, u32[]{:S(2)}) collective-permute-start(f32[3,128,128]{2,1,0:T(8,128)S(1)} %get-tuple-element.17), channel_id=1, source_target_pairs={{0,32},{16,48},{32,0},{48,16},{1,33},{17,49},{33,1},{49,17},{2,34}... | collective-permute-start | bytes 589832 | tf_op jit(solution)/shard_map/ppermute | solution.py:232
  13.0 27.1 %collective-permute-start.5 = (f32[3,128,128]{2,1,0:T(8,128)S(1)}, f32[3,128,128]{2,1,0:T(8,128)S(1)}, u32[]{:S(2)}, u32[]{:S(2)}) collective-permute-start(f32[3,128,128]{2,1,0:T(8,128)S(1)} %get-tuple-element.18), channel_id=1, source_target_pairs={{0,16},{16,32},{32,48},{48,0},{1,17},{17,33},{33,49},{49,1},{2,18}... | collective-permute-start | bytes 589832 | tf_op jit(solution)/shard_map/ppermute | solution.py:232
  15.9 12.3 %copy-start.5 = (f32[1,2,128,128]{3,2,1,0:T(8,128)}, f32[1,2,128,128]{3,2,1,0:T(8,128)S(1)}, u32[]{:S(2)}) copy-start(f32[1,2,128,128]{3,2,1,0:T(8,128)S(1)} %collective-permute-done.1.third) | copy-start | bytes 393220
  15.9 12.3 %collective-permute-start.2 = (f32[1,2,128,128]{3,2,1,0:T(8,128)S(1)}, f32[1,2,128,128]{3,2,1,0:T(8,128)S(1)}, u32[]{:S(2)}, u32[]{:S(2)}) collective-permute-start(f32[1,2,128,128]{3,2,1,0:T(8,128)S(1)} %collective-permute-done.1.third), channel_id=1, source_target_pairs={{0,64},{64,0},{1,65},{65,1},{2,66},{66,2},{3,67},{67,3},{4,68},{68... | collective-permute-start | bytes 393224 | tf_op jit(solution)/shard_map/ppermute | solution.py:195
  29.6 0.7 copy-start.7
  30.3 0.6 copy-start.9
  30.9 29.5 %all-to-all-start = ((f32[16,8,1,8,128]{4,3,2,1,0:T(8,128)}), f32[16,8,1,8,128]{4,3,2,1,0:T(8,128)S(1)}, u32[]{:S(2)}, u32[]{:S(2)}) async-start(f32[16,8,1,8,128]{4,3,2,1,0:T(8,128)} %forward_planes.2), calls=%async_computation | async-start | bytes 1048576 | tf_op jit(solution)/shard_map/all_to_all | solution.py:191
  40.2 15.4 %collective-permute-start.7 = (f32[3,2,128,128]{3,2,1,0:T(8,128)S(1)}, f32[3,2,128,128]{3,2,1,0:T(8,128)S(1)}, u32[]{:S(2)}, u32[]{:S(2)}) collective-permute-start(f32[3,2,128,128]{3,2,1,0:T(8,128)S(1)} %pad_maximum_fusion.own), channel_id=1, source_target_pairs={{0,128},{128,0},{1,129},{129,1},{2,130},{130,2},{3,131},{131,3},{4... | collective-permute-start | bytes 1179656 | tf_op jit(solution)/shard_map/ppermute | solution.py:195
  40.8 14.9 %collective-permute-start.6 = (f32[3,2,128,128]{3,2,1,0:T(8,128)S(1)}, f32[3,2,128,128]{3,2,1,0:T(8,128)S(1)}, u32[]{:S(2)}, u32[]{:S(2)}) collective-permute-start(f32[3,2,128,128]{3,2,1,0:T(8,128)S(1)} %pad_maximum_fusion.own), channel_id=1, source_target_pairs={{0,64},{64,0},{1,65},{65,1},{2,66},{66,2},{3,67},{67,3},{4,68},{68... | collective-permute-start | bytes 1179656 | tf_op jit(solution)/shard_map/ppermute | solution.py:195
  55.6 1.7 %collective-permute-start.8 = (f32[3,2,128,128]{3,2,1,0:T(8,128)S(1)}, f32[3,2,128,128]{3,2,1,0:T(8,128)S(1)}, u32[]{:S(2)}, u32[]{:S(2)}) collective-permute-start(f32[3,2,128,128]{3,2,1,0:T(8,128)S(1)} %collective-permute-done.7.third), channel_id=1, source_target_pairs={{0,64},{64,0},{1,65},{65,1},{2,66},{66,2},{3,67},{67,3},{4,68},{68... | collective-permute-start | bytes 1179656 | tf_op jit(solution)/shard_map/ppermute | solution.py:195
  59.7 0.8 copy-start
  60.5 33.7 %copy-start.15 = (f32[64,128]{1,0:T(8,128)S(1)}, f32[64,128]{1,0:T(8,128)}, u32[]{:S(2)}) copy-start(f32[64,128]{1,0:T(8,128)} %constant.80.clone.squares) | copy-start | bytes 98308
  60.5 33.7 %copy-start.16 = (bf16[64,192]{1,0:T(8,128)(2,1)S(1)}, bf16[64,192]{1,0:T(8,128)(2,1)}, u32[]{:S(2)}) copy-start(bf16[64,192]{1,0:T(8,128)(2,1)} %constant.78.clone.back) | copy-start | bytes 73732
  60.5 33.7 %copy-start.17 = (bf16[64,192]{1,0:T(8,128)(2,1)S(1)}, bf16[64,192]{1,0:T(8,128)(2,1)}, u32[]{:S(2)}) copy-start(bf16[64,192]{1,0:T(8,128)(2,1)} %constant.77.clone.ahead) | copy-start | bytes 73732
  60.5 33.6 %all-to-all-start.1 = ((f32[16,8,3,8,128]{4,3,2,1,0:T(8,128)}), f32[16,8,3,8,128]{4,3,2,1,0:T(8,128)S(1)}, u32[]{:S(2)}, u32[]{:S(2)}) async-start(f32[16,8,3,8,128]{4,3,2,1,0:T(8,128)} %forward_planes.3), calls=%async_computation.1 | async-start | bytes 3145728 | tf_op jit(solution)/shard_map/all_to_all | solution.py:191
  97.3 28.0 %copy-start.4 = (f32[16,8,1,8,128]{4,3,2,1,0:T(8,128)}, f32[16,8,1,8,128]{4,3,2,1,0:T(8,128)S(1)}, u32[]{:S(2)}) copy-start(f32[16,8,1,8,128]{4,3,2,1,0:T(8,128)S(1)} %get-tuple-element.7) | copy-start | bytes 1572868
  97.3 33.3 %copy-start.2 = (bf16[256,256]{1,0:T(8,128)(2,1)S(1)}, bf16[256,256]{1,0:T(8,128)(2,1)}, u32[]{:S(2)}) copy-start(bf16[256,256]{1,0:T(8,128)(2,1)} %constant.75.clone.right) | copy-start | bytes 393220
  125.3 15.4 %all-to-all-start.2 = ((f32[16,8,1,8,128]{4,3,2,1,0:T(8,128)}), f32[16,8,1,8,128]{4,3,2,1,0:T(8,128)S(1)}, u32[]{:S(2)}, u32[]{:S(2)}) async-start(f32[16,8,1,8,128]{4,3,2,1,0:T(8,128)} %copy-done.4), calls=%async_computation.2 | async-start | bytes 1048576 | tf_op jit(solution)/shard_map/all_to_all | solution.py:191
  130.6 1.0 copy-start.1
  131.6 0.9 copy-start.11
  133.6 11.2 %collective-permute-start.9 = (f32[128,128]{1,0:T(8,128)S(1)}, f32[128,128]{1,0:T(8,128)S(1)}, u32[]{:S(2)}, u32[]{:S(2)}) collective-permute-start(f32[128,128]{1,0:T(8,128)S(1)} %get-tuple-element.13), channel_id=1, source_target_pairs={{0,16},{16,32},{32,48},{48,0},{1,17},{17,33},{33,49},{49,1},{2,18}... | collective-permute-start | bytes 196616 | tf_op jit(solution)/shard_map/ppermute | solution.py:246
  133.7 11.1 %collective-permute-start.11 = (f32[128,128]{1,0:T(8,128)S(1)}, f32[128,128]{1,0:T(8,128)S(1)}, u32[]{:S(2)}, u32[]{:S(2)}) collective-permute-start(f32[128,128]{1,0:T(8,128)S(1)} %get-tuple-element.14), channel_id=1, source_target_pairs={{0,48},{16,0},{32,16},{48,32},{1,49},{17,1},{33,17},{49,33},{2,50}... | collective-permute-start | bytes 196616 | tf_op jit(solution)/shard_map/ppermute | solution.py:246
  137.9 8.8 %collective-permute-start.10 = (f32[128,128]{1,0:T(8,128)S(1)}, f32[128,128]{1,0:T(8,128)S(1)}, u32[]{:S(2)}, u32[]{:S(2)}) collective-permute-start(f32[128,128]{1,0:T(8,128)S(1)} %get-tuple-element.15), channel_id=1, source_target_pairs={{0,32},{16,48},{32,0},{48,16},{1,33},{17,49},{33,1},{49,17},{2,34}... | collective-permute-start | bytes 196616 | tf_op jit(solution)/shard_map/ppermute | solution.py:246
  140.7 0.9 copy-start.6
  141.6 0.9 copy-start.8
  142.5 0.9 copy-start.10
  143.4 0.9 copy-start.12
where the time goes:
time: 148 us; the launch traced here: 147 us
  waiting for transfers between devices  55.2 us (37%)
  starting transfers between devices  42.2 us (29%)
  blocking collectives  28 us (19%)
  local copies, waits for them, and re-layouts  9.47 us (6%)
  Pallas kernels  8.62 us (6%)
  other arithmetic  2.92 us (2%)
    all_to_all x1, blocking collectives, exchange(): return lax.all_to_all(value, SPREAD, 0, 0, tiled=True)  28 us
    all_to_all x3, waiting for transfers between devices, exchange(): return lax.all_to_all(value, SPREAD, 0, 0, tiled=True)  24.6 us
    all_to_all x3, starting transfers between devices, exchange(): return lax.all_to_all(value, SPREAD, 0, 0, tiled=True)  22.9 us
    ppermute x6, waiting for transfers between devices, swap(): return lax.ppermute(value, axis, [(0, 1), (1, 0)])  16.5 us
    ppermute x3, waiting for transfers between devices, local(): arrived.append(lax.ppermute(packet, 'zh', perm))  12.2 us
    ppermute x3, starting transfers between devices, local(): arrived.append(lax.ppermute(packet, 'zh', perm))  10.2 us
    unnamed x36, local copies, waits for them, and re-layouts  7.58 us
    ppermute x3, starting transfers between devices, local(): returned.append(lax.ppermute(rest[step - 1], 'zh', perm))  7.01 us
  transfers between devices with their start and end apart: 15, of which 6 were waited for; matrix products, arithmetic and copies ran while one was open for 1% of the time, Pallas kernels for 4%

commit v1 on v0

v1 whole, which is shorter than its diff:
```python
import math

import jax
import jax.numpy as jnp
import ml_dtypes
import numpy as np
from jax import lax
from jax.experimental import pallas as pl
from jax.experimental.pallas import tpu as pltpu
from jax.sharding import Mesh, PartitionSpec as P

BLOCK = 8
NX, NY, NZ = 64, 128, 128
AXES = ("yl", "c", "zh", "z0", "x", "yh")
SIZES = (2, 2, 4, 2, 4, 2)
SPREAD = ("z0", "x", "yh")
FAR = 4
SHARE = 16
ROWS = NY // SHARE
KEEP = BLOCK // FAR
VMEM = 16 << 20


def frequencies(length):
    index = np.arange(length)
    return np.where(index <= length // 2, index, index - length // 2)


def basis(length):
    index = np.arange(length)
    freq = frequencies(length)
    angle = 2.0 * np.pi / length * (freq[:, None] * index[None, :] % length)
    rows = np.where((index <= length // 2)[:, None], np.cos(angle), np.sin(angle))
    scale = np.where((index == 0) | (index == length // 2), 1.0, 2.0) / length
    return rows * np.sqrt(scale)[:, None]


def halves(table):
    high = table.astype(np.float32).astype(ml_dtypes.bfloat16)
    low = (table - high.astype(np.float64)).astype(ml_dtypes.bfloat16)
    return high, low


def right_table(table):
    high, low = halves(table)
    return np.concatenate(
        [np.concatenate([high, low], 1), np.concatenate([high, np.zeros_like(low)], 1)], 0
    )


def left_table(table):
    high, low = halves(table)
    return np.concatenate([high, high, low], 1)


def split(value):
    high = value.astype(jnp.bfloat16)
    low = (value - high.astype(jnp.float32)).astype(jnp.bfloat16)
    return high, low


def times_right(value, table):
    high, low = split(value)
    both = jnp.dot(
        jnp.concatenate([high, low], axis=1), table, preferred_element_type=jnp.float32
    )
    size = both.shape[1] // 2
    return both[:, :size] + both[:, size:]


def times_left(table, value):
    high, low = split(value)
    return jnp.dot(
        table, jnp.concatenate([high, low, high], axis=0), preferred_element_type=jnp.float32
    )


def forward_kernel(*refs):
    trials, bands = refs[:FAR], refs[FAR : FAR + 4]
    right, left, out = refs[FAR + 4 :]
    for plane in range(FAR):
        for slot, block in enumerate(bands):
            pair = jnp.concatenate(
                [trials[plane][0] * block[plane, k] for k in range(KEEP)], axis=0
            )
            pair = times_right(pair, right[...])
            pair = jnp.concatenate([pair[:NY], pair[NY:]], axis=1)
            pair = times_left(left[...], pair)
            for k in range(KEEP):
                out[:, slot * KEEP + k, plane] = pair[:, k * NZ : (k + 1) * NZ].reshape(
                    SHARE, ROWS, NZ
                )


def inverse_kernel(potential, own, second, third, fourth, right, left, *outs):
    for plane in range(FAR):
        total = jnp.zeros((NY, NZ), jnp.float32)
        for slot, bands in enumerate((own, second, third, fourth)):
            pair = jnp.concatenate(
                [potential[:, slot * KEEP + k, plane].reshape(NY, NZ) for k in range(KEEP)],
                axis=1,
            )
            pair = times_left(left[...], pair)
            pair = jnp.concatenate([pair[:, :NZ], pair[:, NZ:]], axis=0)
            pair = times_right(pair, right[...])
            total = total + pair[:NY] * bands[plane, 0] + pair[NY:] * bands[plane, 1]
        outs[plane][...] = total * (-math.sqrt(NX * NY * NZ) / BLOCK)


def solve_kernel(spectrum, squares, base, ahead, back, out):
    bands = spectrum.shape[1]
    for row in range(ROWS):
        kernel = 1.0 / (squares[...] + base[row : row + 1, :])
        kernel = jnp.concatenate([kernel, kernel], axis=1)
        for band in range(0, bands, 2):
            columns = jnp.concatenate(
                [
                    jnp.concatenate([spectrum[:, b, p, row, :] for p in range(FAR)], axis=0)
                    for b in (band, band + 1)
                ],
                axis=1,
            )
            columns = times_left(ahead[...], columns) * kernel
            columns = times_left(back[...], columns)
            for i in range(2):
                part = columns[:, i * NZ : (i + 1) * NZ]
                for p in range(FAR):
                    out[:, band + i, p, row, :] = part[p * SHARE : (p + 1) * SHARE]


def params():
    return pltpu.CompilerParams(vmem_limit_bytes=VMEM)


def specs(count):
    return [pl.BlockSpec(memory_space=pltpu.VMEM)] * count


def cost():
    return pl.CostEstimate(
        flops=FAR * 8 * 128 * 128 * 256 * 6, bytes_accessed=4 << 20, transcendentals=0
    )


def forward(trials, bands, right, left):
    shape = (SHARE, 4 * KEEP, FAR, ROWS, NZ)
    return pl.pallas_call(
        forward_kernel,
        out_shape=jax.ShapeDtypeStruct(shape, jnp.float32),
        in_specs=specs(FAR + 6),
        out_specs=specs(1)[0],
        compiler_params=params(),
        cost_estimate=cost(),
        name="forward_planes",
    )(*trials, *bands, right, left)


def inverse(potential, bands, right, left):
    return pl.pallas_call(
        inverse_kernel,
        out_shape=[jax.ShapeDtypeStruct((NY, NZ), jnp.float32)] * FAR,
        in_specs=specs(7),
        out_specs=specs(FAR),
        compiler_params=params(),
        cost_estimate=cost(),
        name="inverse_planes",
    )(potential, *bands, right, left)


def solve(spectrum, squares, base, ahead, back):
    return pl.pallas_call(
        solve_kernel,
        out_shape=jax.ShapeDtypeStruct(spectrum.shape, jnp.float32),
        in_specs=specs(5),
        out_specs=specs(1)[0],
        compiler_params=params(),
        cost_estimate=cost(),
        name="solve_columns",
    )(spectrum, squares, base, ahead, back)


def exchange(value):
    return lax.all_to_all(value, SPREAD, 0, 0, tiled=True)


def swap(value, axis):
    return lax.ppermute(value, axis, [(0, 1), (1, 0)])


def local(orbitals, trials, owner_group, block_index):
    plane_table = basis(NY)
    column_table = basis(NX)
    right_ahead = jnp.asarray(right_table(plane_table.T))
    left_ahead = jnp.asarray(left_table(plane_table))
    right_back = jnp.asarray(right_table(plane_table))
    left_back = jnp.asarray(left_table(plane_table.T))
    column_ahead = jnp.asarray(left_table(column_table))
    column_back = jnp.asarray(left_table(column_table.T))
    squares = np.broadcast_to((frequencies(NX)[:, None] ** 2), (NX, NZ)).astype(np.float32)
    grid_squares = 1 + frequencies(NY)[:, None] ** 2 + frequencies(NZ)[None, :] ** 2
    base = lax.dynamic_slice_in_dim(
        jnp.asarray(grid_squares.astype(np.float32)), lax.axis_index(SPREAD) * ROWS, ROWS, 0
    )

    group = lax.axis_index(("yl", "c"))
    mine = jnp.sum(jnp.where(owner_group == group, block_index, 0)) * BLOCK
    far = lax.axis_index("zh")

    def bands_for(place):
        start = mine + lax.rem(place + FAR, FAR) * KEEP
        return lax.dynamic_slice_in_dim(orbitals[:, 0], start, KEEP, 0)

    trial = trials[0]
    steps = range(1, FAR)
    there = [[(i, (i - step) % FAR) for i in range(FAR)] for step in steps]
    back = [[(i, (i + step) % FAR) for i in range(FAR)] for step in steps]
    own = jnp.stack(
        [bands_for(far)]
        + [lax.ppermute(bands_for(far - step), "zh", there[step - 1]) for step in steps]
    )
    own, trial = lax.optimization_barrier((own, trial))
    across = swap(own, "yl")
    trial_planes = [lax.ppermute(trial, "zh", perm) for perm in there]
    across, trial_planes = lax.optimization_barrier((across, trial_planes))
    bands = (own, swap(own, "c"), across, swap(across, "c"))
    spectrum = forward([trial] + trial_planes, bands, right_ahead, left_ahead)
    spectrum, base = lax.optimization_barrier((spectrum, base))
    spectrum = solve(
        exchange(spectrum), jnp.asarray(squares), base, column_ahead, column_back
    )
    planes = inverse(exchange(spectrum), bands, right_back, left_back)
    total = planes[0]
    for plane, perm in zip(planes[1:], back):
        total = total + lax.ppermute(plane, "zh", perm)
    return total[None, None]


def solution(mesh):
    fine = Mesh(mesh.devices.reshape(SIZES), AXES)
    spec = P(("yl", "c"), ("zh", "z0", "x", "yh"), None, None)
    return jax.shard_map(
        local,
        mesh=fine,
        in_specs=(spec, spec, P(), P()),
        out_specs=spec,
        check_vma=False,
    )
```

time: 148 us -> 127 us (0.86)
  blocking collectives: 28 us -> 68.7 us
  waiting for transfers between devices: 55.2 us -> 21.3 us
  starting transfers between devices: 42.2 us -> 25.7 us
  local copies, waits for them, and re-layouts: 9.47 us -> 1.87 us
  Pallas kernels: 8.62 us -> 6.57 us
    all_to_all x1 -> x2, blocking collectives: 28 us -> 68.7 us  [exchange(): return lax.all_to_all(value, SPREAD, 0, 0, tiled=True)]
    all_to_all x3 -> x0, waiting for transfers between devices: 24.6 us -> none  [exchange(): return lax.all_to_all(value, SPREAD, 0, 0, tiled=True)]
    all_to_all x3 -> x0, starting transfers between devices: 22.9 us -> none  [exchange(): return lax.all_to_all(value, SPREAD, 0, 0, tiled=True)]
    ppermute x6 -> x3, waiting for transfers between devices: 16.5 us -> 1.22 us  [swap(): return lax.ppermute(value, axis, [(0, 1), (1, 0)])]
    unnamed x36 -> x16, local copies, waits for them, and re-layouts: 7.58 us -> 0.05 us
    ppermute x6 -> x9, starting transfers between devices: 17.2 us -> 24 us  [the longest x3 10.2 us: local(): lax.ppermute(bands_for(far - step), 'zh', there[step - 1])]
    ppermute x6 -> x9, waiting for transfers between devices: 14 us -> 20.1 us  [the longest x3 9.39 us: local(): lax.ppermute(bands_for(far - step), 'zh', there[step - 1])]
    pallas_call x2 -> x1, Pallas kernels: 3.77 us -> 1.44 us  [forward(): pl.pallas_call(forward_kernel, out_shape=jax.ShapeDtypeStruct(shape, jnp....]
  transfers between devices with their start and end apart: 15 -> 12, of which waited for: 6 -> 8; matrix products, arithmetic and copies ran while one was open for 1% -> 1% of each run, Pallas kernels for 4% -> 0%
where the time goes in v1:
time: 127 us
  blocking collectives  68.7 us (54%)
  starting transfers between devices  25.7 us (20%)
  waiting for transfers between devices  21.3 us (17%)
  Pallas kernels  6.57 us (5%)
  other arithmetic  2.04 us (2%)
  local copies, waits for them, and re-layouts  1.87 us (1%)
    all_to_all x2, blocking collectives, exchange(): return lax.all_to_all(value, SPREAD, 0, 0, tiled=True)  68.7 us
    ppermute x3, starting transfers between devices, local(): lax.ppermute(bands_for(far - step), 'zh', there[step - 1])  10.2 us
    ppermute x3, waiting for transfers between devices, local(): lax.ppermute(bands_for(far - step), 'zh', there[step - 1])  9.39 us
    ppermute x3, starting transfers between devices, local(): trial_planes = [lax.ppermute(trial, 'zh', perm) for perm in there]  7.74 us
    ppermute x3, starting transfers between devices, local(): total = total + lax.ppermute(plane, 'zh', perm)  6.11 us
    ppermute x3, waiting for transfers between devices, local(): total = total + lax.ppermute(plane, 'zh', perm)  5.96 us
    ppermute x3, waiting for transfers between devices, local(): trial_planes = [lax.ppermute(trial, 'zh', perm) for perm in there]  4.76 us
    pallas_call x1, Pallas kernels, solve(): pl.pallas_call(solve_kernel, out_shape=jax.ShapeDtypeStruct(spectrum.shap...  3.71 us
  transfers between devices with their start and end apart: 12, of which 8 were waited for; matrix products, arithmetic and copies ran while one was open for 1% of the time, Pallas kernels for 0%

profile of v1, /device:TPU:2, one launch (start us, length us, event | category | flops | bytes accessed | tf_op | source)
XLA Modules:
  0.0 127.0 jit_solution(16843256297329198670)
XLA Ops:
  0.0 0.0 copy-start.3
  0.0 0.0 copy-start.1
  0.0 0.0 copy-start.4
  0.0 1.4 %fusion = s32[]{:T(128)} fusion(s32[4]{0:T(128)} %param.15, s32[4]{0:T(128)} %param.14, s32[]{:T(128)S(6)} %add.66), kind=kLoop, calls=%fused_computation.8 | loop fusion | flops 11 | bytes 40 | tf_op jit(solution)/shard_map/reduce_sum | solution.py:206
  2.1 1.1 dynamic-slice_bitcast_fusion.3
  3.2 6.4 %collective-permute-start = (f32[2,128,128]{2,1,0:T(8,128)S(1)}, f32[2,128,128]{2,1,0:T(8,128)S(1)}, u32[]{:S(2)}, u32[]{:S(2)}) collective-permute-start(f32[2,128,128]{2,1,0:T(8,128)S(1)} %get-tuple-element.30), channel_id=1, source_target_pairs={{0,48},{16,0},{32,16},{48,32},{1,49},{17,1},{33,17},{49,33},{2,50}... | collective-permute-start | bytes 393224 | tf_op jit(solution)/shard_map/ppermute | solution.py:219
  9.6 0.0 collective-permute-start.2
  9.6 3.8 %collective-permute-start.1 = (f32[2,128,128]{2,1,0:T(8,128)S(1)}, f32[2,128,128]{2,1,0:T(8,128)S(1)}, u32[]{:S(2)}, u32[]{:S(2)}) collective-permute-start(f32[2,128,128]{2,1,0:T(8,128)S(1)} %get-tuple-element.32), channel_id=1, source_target_pairs={{0,32},{16,48},{32,0},{48,16},{1,33},{17,49},{33,1},{49,17},{2,34}... | collective-permute-start | bytes 393224 | tf_op jit(solution)/shard_map/ppermute | solution.py:219
  13.4 6.8 %collective-permute-done = f32[2,128,128]{2,1,0:T(8,128)S(1)} collective-permute-done((f32[2,128,128]{2,1,0:T(8,128)S(1)}, f32[2,128,128]{2,1,0:T(8,128)S(1)}, u32[]{:S(2)}, u32[]{:S(2)}) %collective-permute-start) | collective-permute-done | bytes 131104 | tf_op jit(solution)/shard_map/ppermute | solution.py:219
  20.2 2.6 %collective-permute-done.2 = f32[2,128,128]{2,1,0:T(8,128)S(1)} collective-permute-done((f32[2,128,128]{2,1,0:T(8,128)S(1)}, f32[2,128,128]{2,1,0:T(8,128)S(1)}, u32[]{:S(2)}, u32[]{:S(2)}) %collective-permute-start.2) | collective-permute-done | bytes 131104 | tf_op jit(solution)/shard_map/ppermute | solution.py:219
  22.8 0.0 collective-permute-done.1
  22.8 1.7 %collective-permute-start.3 = (f32[4,2,128,128]{3,2,1,0:T(8,128)S(1)}, f32[4,2,128,128]{3,2,1,0:T(8,128)S(1)}, u32[]{:S(2)}, u32[]{:S(2)}) collective-permute-start(f32[4,2,128,128]{3,2,1,0:T(8,128)S(1)} %pad_maximum_fusion.refs_4_.own), channel_id=1, source_target_pairs={{0,128},{128,0},{1,129},{129,1},{2,130},{130,2},{3,131},{131,3},{4... | collective-permute-start | bytes 1572872 | tf_op jit(solution)/shard_map/ppermute | solution.py:187
  24.5 0.0 copy-done.4
  24.5 4.2 %collective-permute-start.6 = (f32[1,128,128]{2,1,0:T(8,128)S(1)}, f32[1,128,128]{2,1,0:T(8,128)S(1)}, u32[]{:S(2)}, u32[]{:S(2)}) collective-permute-start(f32[1,128,128]{2,1,0:T(8,128)S(1)} %bitcast.14), channel_id=1, source_target_pairs={{0,16},{16,32},{32,48},{48,0},{1,17},{17,33},{33,49},{49,1},{2,18}... | collective-permute-start | bytes 196616 | tf_op jit(solution)/shard_map/ppermute | solution.py:223
  28.7 2.1 %collective-permute-start.5 = (f32[1,128,128]{2,1,0:T(8,128)S(1)}, f32[1,128,128]{2,1,0:T(8,128)S(1)}, u32[]{:S(2)}, u32[]{:S(2)}) collective-permute-start(f32[1,128,128]{2,1,0:T(8,128)S(1)} %bitcast.15), channel_id=1, source_target_pairs={{0,32},{16,48},{32,0},{48,16},{1,33},{17,49},{33,1},{49,17},{2,34}... | collective-permute-start | bytes 196616 | tf_op jit(solution)/shard_map/ppermute | solution.py:223
  30.8 1.5 %collective-permute-start.4 = (f32[1,128,128]{2,1,0:T(8,128)S(1)}, f32[1,128,128]{2,1,0:T(8,128)S(1)}, u32[]{:S(2)}, u32[]{:S(2)}) collective-permute-start(f32[1,128,128]{2,1,0:T(8,128)S(1)} %bitcast.16), channel_id=1, source_target_pairs={{0,48},{16,0},{32,16},{48,32},{1,49},{17,1},{33,17},{49,33},{2,50}... | collective-permute-start | bytes 196616 | tf_op jit(solution)/shard_map/ppermute | solution.py:223
  32.2 0.0 collective-permute-start.7
  32.2 0.0 collective-permute-done.6.refs_3_
  32.3 4.7 %collective-permute-done.5.refs_2_ = f32[1,128,128]{2,1,0:T(8,128)S(1)} collective-permute-done((f32[1,128,128]{2,1,0:T(8,128)S(1)}, f32[1,128,128]{2,1,0:T(8,128)S(1)}, u32[]{:S(2)}, u32[]{:S(2)}) %collective-permute-start.5) | collective-permute-done | bytes 65568 | tf_op jit(solution)/shard_map/ppermute | solution.py:223
  37.0 0.1 collective-permute-done.4.refs_1_
  37.0 0.0 collective-permute-done.3.refs_6_.third
  37.0 0.0 collective-permute-start.8
  37.0 0.7 constant_dynamic-slice_fusion.base
  37.7 0.0 collective-permute-done.7.refs_5_.second
  37.7 1.2 collective-permute-done.8.refs_7_.fourth
  38.9 0.0 copy-done.3
  38.9 0.0 copy-done.1
  38.9 1.4 %forward_planes.1 = f32[16,8,4,8,128]{4,3,2,1,0:T(8,128)S(1)} custom-call(f32[1,128,128]{2,1,0:T(8,128)S(1)} %bitcast.17, f32[1,128,128]{2,1,0:T(8,128)S(1)} %collective-permute-done.4.refs_1_, f32[1,128,128]{2,1,0:T(8,128)S(1)} %collective-permute-done.5.refs_2_, f32[1,128,128]{2,1,0:T(8,128)S(1)} %collective-permute-done.6.refs_3_, ...), custom_call_target="tpu_custom_call" | custom-call | flops 805306368 | bytes 4194304 | tf_op jit(solution)/shard_map/forward_planes/pallas_call | solution.py:147
  40.4 0.0 copy-start.5
  40.4 0.0 copy-start.6
  40.4 0.0 copy-start.7
  40.4 36.1 %all_to_all.10.spectrum = f32[16,8,4,8,128]{4,3,2,1,0:T(8,128)S(1)} all-to-all(f32[16,8,4,8,128]{4,3,2,1,0:T(8,128)S(1)} %forward_planes.1), channel_id=1, replica_groups=mesh['yl'=2,'c'=2,'zh'=4,'z0'=2,'x'=4,'yh'=2] {'z0','x','yh'}, dimensions={0} | all-to-all | bytes 4194304 | tf_op jit(solution)/shard_map/all_to_all | solution.py:183
  76.5 0.0 copy-done.5
  76.5 0.0 copy-done.6
  76.5 0.0 copy-done.7
  76.5 3.7 %solve_columns.1 = f32[16,8,4,8,128]{4,3,2,1,0:T(8,128)S(1)} custom-call(f32[16,8,4,8,128]{4,3,2,1,0:T(8,128)S(1)} %all_to_all.10.spectrum, f32[64,128]{1,0:T(8,128)S(1)} %copy-done.5, f32[8,128]{1,0:T(8,128)S(1)} %constant_dynamic-slice_fusion.base, bf16[64,192]{1,0:T(8,128)(2,1)S(1)} %copy-done.7, bf16[64,192]{1,0:T(8,128)(2,1)S(1)} %copy-done.6), custom_call_target="tpu_custom_call" | custom-call | flops 805306368 | bytes 4194304 | tf_op jit(solution)/shard_map/solve_columns/pallas_call | solution.py:171
  80.2 0.0 copy-start
  80.2 0.0 copy-start.2
  80.3 32.6 %all_to_all.11.potential = f32[16,8,4,8,128]{4,3,2,1,0:T(8,128)S(1)} all-to-all(f32[16,8,4,8,128]{4,3,2,1,0:T(8,128)S(1)} %solve_columns.1), channel_id=1, replica_groups=mesh['yl'=2,'c'=2,'zh'=4,'z0'=2,'x'=4,'yh'=2] {'z0','x','yh'}, dimensions={0} | all-to-all | bytes 4194304 | tf_op jit(solution)/shard_map/all_to_all | solution.py:183
  112.9 0.0 copy-done
  112.9 0.0 copy-done.2
  112.9 1.4 %inverse_planes.1 = (f32[128,128]{1,0:T(8,128)S(1)}, f32[128,128]{1,0:T(8,128)S(1)}, f32[128,128]{1,0:T(8,128)S(1)}, f32[128,128]{1,0:T(8,128)S(1)}) custom-call(f32[16,8,4,8,128]{4,3,2,1,0:T(8,128)S(1)} %all_to_all.11.potential, f32[4,2,128,128]{3,2,1,0:T(8,128)S(1)} %pad_maximum_fusion.refs_4_.own, ...), custom_call_target="tpu_custom_call" | custom-call | flops 805306368 | bytes 4194304 | tf_op jit(solution)/shard_map/inverse_planes/pallas_call | solution.py:159
  114.3 2.4 %collective-permute-start.9 = (f32[128,128]{1,0:T(8,128)S(1)}, f32[128,128]{1,0:T(8,128)S(1)}, u32[]{:S(2)}, u32[]{:S(2)}) collective-permute-start(f32[128,128]{1,0:T(8,128)S(1)} %get-tuple-element.26), channel_id=1, source_target_pairs={{0,16},{16,32},{32,48},{48,0},{1,17},{17,33},{33,49},{49,1},{2,18}... | collective-permute-start | bytes 196616 | tf_op jit(solution)/shard_map/ppermute | solution.py:234
  116.8 2.9 %collective-permute-start.10 = (f32[128,128]{1,0:T(8,128)S(1)}, f32[128,128]{1,0:T(8,128)S(1)}, u32[]{:S(2)}, u32[]{:S(2)}) collective-permute-start(f32[128,128]{1,0:T(8,128)S(1)} %get-tuple-element.27), channel_id=1, source_target_pairs={{0,32},{16,48},{32,0},{48,16},{1,33},{17,49},{33,1},{49,17},{2,34}... | collective-permute-start | bytes 196616 | tf_op jit(solution)/shard_map/ppermute | solution.py:234
  119.6 0.8 collective-permute-start.11
  120.4 1.6 %collective-permute-done.9 = f32[128,128]{1,0:T(8,128)S(1)} collective-permute-done((f32[128,128]{1,0:T(8,128)S(1)}, f32[128,128]{1,0:T(8,128)S(1)}, u32[]{:S(2)}, u32[]{:S(2)}) %collective-permute-start.9) | collective-permute-done | bytes 65568 | tf_op jit(solution)/shard_map/ppermute | solution.py:234
  122.1 2.9 %collective-permute-done.10 = f32[128,128]{1,0:T(8,128)S(1)} collective-permute-done((f32[128,128]{1,0:T(8,128)S(1)}, f32[128,128]{1,0:T(8,128)S(1)}, u32[]{:S(2)}, u32[]{:S(2)}) %collective-permute-start.10) | collective-permute-done | bytes 65568 | tf_op jit(solution)/shard_map/ppermute | solution.py:234
  124.9 1.5 %collective-permute-done.11 = f32[128,128]{1,0:T(8,128)S(1)} collective-permute-done((f32[128,128]{1,0:T(8,128)S(1)}, f32[128,128]{1,0:T(8,128)S(1)}, u32[]{:S(2)}, u32[]{:S(2)}) %collective-permute-start.11) | collective-permute-done | bytes 65568 | tf_op jit(solution)/shard_map/ppermute | solution.py:234
  126.4 0.6 add_bitcast_fusion
  (1 shorter events, 0.0 us)
Async XLA Ops:
  0.0 38.9 %copy-start.3 = (bf16[128,384]{1,0:T(8,128)(2,1)S(1)}, bf16[128,384]{1,0:T(8,128)(2,1)}, u32[]{:S(2)}) copy-start(bf16[128,384]{1,0:T(8,128)(2,1)} %constant.74.clone.refs_9_) | copy-start | bytes 294916
  0.0 38.9 %copy-start.1 = (bf16[256,256]{1,0:T(8,128)(2,1)S(1)}, bf16[256,256]{1,0:T(8,128)(2,1)}, u32[]{:S(2)}) copy-start(bf16[256,256]{1,0:T(8,128)(2,1)} %constant.73.clone.refs_8_) | copy-start | bytes 393220
  0.0 24.5 %copy-start.4 = (f32[1,1,128,128]{3,2,1,0:T(8,128)S(1)}, f32[1,1,128,128]{3,2,1,0:T(8,128)}, u32[]{:S(2)}) copy-start(f32[1,1,128,128]{3,2,1,0:T(8,128)} %param.13) | copy-start | bytes 196612
  3.2 17.0 %collective-permute-start = (f32[2,128,128]{2,1,0:T(8,128)S(1)}, f32[2,128,128]{2,1,0:T(8,128)S(1)}, u32[]{:S(2)}, u32[]{:S(2)}) collective-permute-start(f32[2,128,128]{2,1,0:T(8,128)S(1)} %get-tuple-element.30), channel_id=1, source_target_pairs={{0,48},{16,0},{32,16},{48,32},{1,49},{17,1},{33,17},{49,33},{2,50}... | collective-permute-start | bytes 393224 | tf_op jit(solution)/shard_map/ppermute | solution.py:219
  9.6 13.2 %collective-permute-start.2 = (f32[2,128,128]{2,1,0:T(8,128)S(1)}, f32[2,128,128]{2,1,0:T(8,128)S(1)}, u32[]{:S(2)}, u32[]{:S(2)}) collective-permute-start(f32[2,128,128]{2,1,0:T(8,128)S(1)} %get-tuple-element.31), channel_id=1, source_target_pairs={{0,16},{16,32},{32,48},{48,0},{1,17},{17,33},{33,49},{49,1},{2,18}... | collective-permute-start | bytes 393224 | tf_op jit(solution)/shard_map/ppermute | solution.py:219
  9.6 13.2 %collective-permute-start.1 = (f32[2,128,128]{2,1,0:T(8,128)S(1)}, f32[2,128,128]{2,1,0:T(8,128)S(1)}, u32[]{:S(2)}, u32[]{:S(2)}) collective-permute-start(f32[2,128,128]{2,1,0:T(8,128)S(1)} %get-tuple-element.32), channel_id=1, source_target_pairs={{0,32},{16,48},{32,0},{48,16},{1,33},{17,49},{33,1},{49,17},{2,34}... | collective-permute-start | bytes 393224 | tf_op jit(solution)/shard_map/ppermute | solution.py:219
  22.8 14.2 %collective-permute-start.3 = (f32[4,2,128,128]{3,2,1,0:T(8,128)S(1)}, f32[4,2,128,128]{3,2,1,0:T(8,128)S(1)}, u32[]{:S(2)}, u32[]{:S(2)}) collective-permute-start(f32[4,2,128,128]{3,2,1,0:T(8,128)S(1)} %pad_maximum_fusion.refs_4_.own), channel_id=1, source_target_pairs={{0,128},{128,0},{1,129},{129,1},{2,130},{130,2},{3,131},{131,3},{4... | collective-permute-start | bytes 1572872 | tf_op jit(solution)/shard_map/ppermute | solution.py:187
  24.5 7.7 %collective-permute-start.6 = (f32[1,128,128]{2,1,0:T(8,128)S(1)}, f32[1,128,128]{2,1,0:T(8,128)S(1)}, u32[]{:S(2)}, u32[]{:S(2)}) collective-permute-start(f32[1,128,128]{2,1,0:T(8,128)S(1)} %bitcast.14), channel_id=1, source_target_pairs={{0,16},{16,32},{32,48},{48,0},{1,17},{17,33},{33,49},{49,1},{2,18}... | collective-permute-start | bytes 196616 | tf_op jit(solution)/shard_map/ppermute | solution.py:223
  28.7 8.3 %collective-permute-start.5 = (f32[1,128,128]{2,1,0:T(8,128)S(1)}, f32[1,128,128]{2,1,0:T(8,128)S(1)}, u32[]{:S(2)}, u32[]{:S(2)}) collective-permute-start(f32[1,128,128]{2,1,0:T(8,128)S(1)} %bitcast.15), channel_id=1, source_target_pairs={{0,32},{16,48},{32,0},{48,16},{1,33},{17,49},{33,1},{49,17},{2,34}... | collective-permute-start | bytes 196616 | tf_op jit(solution)/shard_map/ppermute | solution.py:223
  30.8 6.2 %collective-permute-start.4 = (f32[1,128,128]{2,1,0:T(8,128)S(1)}, f32[1,128,128]{2,1,0:T(8,128)S(1)}, u32[]{:S(2)}, u32[]{:S(2)}) collective-permute-start(f32[1,128,128]{2,1,0:T(8,128)S(1)} %bitcast.16), channel_id=1, source_target_pairs={{0,48},{16,0},{32,16},{48,32},{1,49},{17,1},{33,17},{49,33},{2,50}... | collective-permute-start | bytes 196616 | tf_op jit(solution)/shard_map/ppermute | solution.py:223
  32.2 5.5 %collective-permute-start.7 = (f32[4,2,128,128]{3,2,1,0:T(8,128)S(1)}, f32[4,2,128,128]{3,2,1,0:T(8,128)S(1)}, u32[]{:S(2)}, u32[]{:S(2)}) collective-permute-start(f32[4,2,128,128]{3,2,1,0:T(8,128)S(1)} %pad_maximum_fusion.refs_4_.own), channel_id=1, source_target_pairs={{0,64},{64,0},{1,65},{65,1},{2,66},{66,2},{3,67},{67,3},{4,68},{68... | collective-permute-start | bytes 1572872 | tf_op jit(solution)/shard_map/ppermute | solution.py:187
  37.0 1.9 %collective-permute-start.8 = (f32[4,2,128,128]{3,2,1,0:T(8,128)S(1)}, f32[4,2,128,128]{3,2,1,0:T(8,128)S(1)}, u32[]{:S(2)}, u32[]{:S(2)}) collective-permute-start(f32[4,2,128,128]{3,2,1,0:T(8,128)S(1)} %collective-permute-done.3.refs_6_.third), channel_id=1, source_target_pairs={{0,64},{64,0},{1,65},{65,1},{2,66},{66,2},{3,67},{67,3},{4,68},{68... | collective-permute-start | bytes 1572872 | tf_op jit(solution)/shard_map/ppermute | solution.py:187
  40.4 36.1 %copy-start.5 = (f32[64,128]{1,0:T(8,128)S(1)}, f32[64,128]{1,0:T(8,128)}, u32[]{:S(2)}) copy-start(f32[64,128]{1,0:T(8,128)} %constant.80.clone.squares) | copy-start | bytes 98308
  40.4 36.1 %copy-start.6 = (bf16[64,192]{1,0:T(8,128)(2,1)S(1)}, bf16[64,192]{1,0:T(8,128)(2,1)}, u32[]{:S(2)}) copy-start(bf16[64,192]{1,0:T(8,128)(2,1)} %constant.78.clone.back) | copy-start | bytes 73732
  40.4 36.1 %copy-start.7 = (bf16[64,192]{1,0:T(8,128)(2,1)S(1)}, bf16[64,192]{1,0:T(8,128)(2,1)}, u32[]{:S(2)}) copy-start(bf16[64,192]{1,0:T(8,128)(2,1)} %constant.77.clone.ahead) | copy-start | bytes 73732
  80.2 32.7 %copy-start = (bf16[256,256]{1,0:T(8,128)(2,1)S(1)}, bf16[256,256]{1,0:T(8,128)(2,1)}, u32[]{:S(2)}) copy-start(bf16[256,256]{1,0:T(8,128)(2,1)} %constant.75.clone.right) | copy-start | bytes 393220
  80.2 32.7 %copy-start.2 = (bf16[128,384]{1,0:T(8,128)(2,1)S(1)}, bf16[128,384]{1,0:T(8,128)(2,1)}, u32[]{:S(2)}) copy-start(bf16[128,384]{1,0:T(8,128)(2,1)} %constant.76.clone.left) | copy-start | bytes 294916
  114.3 7.7 %collective-permute-start.9 = (f32[128,128]{1,0:T(8,128)S(1)}, f32[128,128]{1,0:T(8,128)S(1)}, u32[]{:S(2)}, u32[]{:S(2)}) collective-permute-start(f32[128,128]{1,0:T(8,128)S(1)} %get-tuple-element.26), channel_id=1, source_target_pairs={{0,16},{16,32},{32,48},{48,0},{1,17},{17,33},{33,49},{49,1},{2,18}... | collective-permute-start | bytes 196616 | tf_op jit(solution)/shard_map/ppermute | solution.py:234
  116.8 8.2 %collective-permute-start.10 = (f32[128,128]{1,0:T(8,128)S(1)}, f32[128,128]{1,0:T(8,128)S(1)}, u32[]{:S(2)}, u32[]{:S(2)}) collective-permute-start(f32[128,128]{1,0:T(8,128)S(1)} %get-tuple-element.27), channel_id=1, source_target_pairs={{0,32},{16,48},{32,0},{48,16},{1,33},{17,49},{33,1},{49,17},{2,34}... | collective-permute-start | bytes 196616 | tf_op jit(solution)/shard_map/ppermute | solution.py:234
  119.6 6.8 %collective-permute-start.11 = (f32[128,128]{1,0:T(8,128)S(1)}, f32[128,128]{1,0:T(8,128)S(1)}, u32[]{:S(2)}, u32[]{:S(2)}) collective-permute-start(f32[128,128]{1,0:T(8,128)S(1)} %get-tuple-element.28), channel_id=1, source_target_pairs={{0,48},{16,0},{32,16},{48,32},{1,49},{17,1},{33,17},{49,33},{2,50}... | collective-permute-start | bytes 196616 | tf_op jit(solution)/shard_map/ppermute | solution.py:234

commit v2 on v1

--- a/solution.py
+++ b/solution.py
@@ -1,3 +1,4 @@
+import functools
 import math
 
 import jax
@@ -18,7 +19,7 @@
 SHARE = 16
 ROWS = NY // SHARE
 KEEP = BLOCK // FAR
-VMEM = 16 << 20
+VMEM = 8 << 20
 
 
 def frequencies(length):
@@ -50,7 +51,7 @@
 
 def left_table(table):
     high, low = halves(table)
-    return np.concatenate([high, high, low], 1)
+    return np.concatenate([np.concatenate([high, high], 1), np.concatenate([low, low], 1)], 0)
 
 
 def split(value):
@@ -70,9 +71,11 @@
 
 def times_left(table, value):
     high, low = split(value)
-    return jnp.dot(
-        table, jnp.concatenate([high, low, high], axis=0), preferred_element_type=jnp.float32
-    )
+    both = jnp.dot(
+        table, jnp.concatenate([high, low], axis=0), preferred_element_type=jnp.float32
+    )
+    size = both.shape[0] // 2
+    return both[:size] + both[size:]
 
 
 def forward_kernel(*refs):
@@ -87,36 +90,49 @@
             pair = jnp.concatenate([pair[:NY], pair[NY:]], axis=1)
             pair = times_left(left[...], pair)
             for k in range(KEEP):
-                out[:, slot * KEEP + k, plane] = pair[:, k * NZ : (k + 1) * NZ].reshape(
+                out[:, (slot * KEEP + k) * FAR + plane] = pair[:, k * NZ : (k + 1) * NZ].reshape(
                     SHARE, ROWS, NZ
                 )
 
 
-def inverse_kernel(potential, own, second, third, fourth, right, left, *outs):
-    for plane in range(FAR):
+def inverse_kernel(first, potential, own, second, third, fourth, right, left, *outs):
+    for index, out in enumerate(outs):
+        plane = first + index
         total = jnp.zeros((NY, NZ), jnp.float32)
         for slot, bands in enumerate((own, second, third, fourth)):
             pair = jnp.concatenate(
-                [potential[:, slot * KEEP + k, plane].reshape(NY, NZ) for k in range(KEEP)],
+                [
+                    potential[:, (slot * KEEP + k) * FAR + plane].reshape(NY, NZ)
+                    for k in range(KEEP)
+                ],
                 axis=1,
             )
             pair = times_left(left[...], pair)
             pair = jnp.concatenate([pair[:, :NZ], pair[:, NZ:]], axis=0)
             pair = times_right(pair, right[...])
             total = total + pair[:NY] * bands[plane, 0] + pair[NY:] * bands[plane, 1]
-        outs[plane][...] = total * (-math.sqrt(NX * NY * NZ) / BLOCK)
-
-
-def solve_kernel(spectrum, squares, base, ahead, back, out):
-    bands = spectrum.shape[1]
-    for row in range(ROWS):
-        kernel = 1.0 / (squares[...] + base[row : row + 1, :])
-        kernel = jnp.concatenate([kernel, kernel], axis=1)
-        for band in range(0, bands, 2):
+        out[...] = total * (-math.sqrt(NX * NY * NZ) / BLOCK)
+
+
+def solve_kernel(spectrum, squares, lanes, ahead, back, out):
+    first = (lax.axis_index("z0") * 8 + lax.axis_index("x") * 2 + lax.axis_index("yh")) * ROWS
+    for pair in range(0, ROWS, 2):
+        kernels = []
+        for row in (pair, pair + 1):
+            index = first + row
+            freq = jnp.where(index <= NY // 2, index, index - NY // 2)
+            square = (freq * freq + 1).astype(jnp.float32)
+            kernels.append(1.0 / (squares[...] + (lanes[...] + square)))
+        kernel = jnp.concatenate(kernels, axis=1)
+        kernel = jnp.concatenate([kernel, kernel], axis=0)
+        for start in range(0, 4 * KEEP * FAR, 2 * FAR):
             columns = jnp.concatenate(
                 [
-                    jnp.concatenate([spectrum[:, b, p, row, :] for p in range(FAR)], axis=0)
-                    for b in (band, band + 1)
+                    jnp.concatenate(
+                        [spectrum[s, start : start + 2 * FAR, row, :] for s in range(SHARE)],
+                        axis=0,
+                    )
+                    for row in (pair, pair + 1)
                 ],
                 axis=1,
             )
@@ -124,8 +140,10 @@
             columns = times_left(back[...], columns)
             for i in range(2):
                 part = columns[:, i * NZ : (i + 1) * NZ]
-                for p in range(FAR):
-                    out[:, band + i, p, row, :] = part[p * SHARE : (p + 1) * SHARE]
+                for s in range(SHARE):
+                    out[s, start : start + 2 * FAR, pair + i, :] = part[
+                        s * 2 * FAR : (s + 1) * 2 * FAR
+                    ]
 
 
 def params():
@@ -143,7 +161,7 @@
 
 
 def forward(trials, bands, right, left):
-    shape = (SHARE, 4 * KEEP, FAR, ROWS, NZ)
+    shape = (SHARE, 4 * KEEP * FAR, ROWS, NZ)
     return pl.pallas_call(
         forward_kernel,
         out_shape=jax.ShapeDtypeStruct(shape, jnp.float32),
@@ -155,19 +173,19 @@
     )(*trials, *bands, right, left)
 
 
-def inverse(potential, bands, right, left):
+def inverse(first, count, potential, bands, right, left):
     return pl.pallas_call(
-        inverse_kernel,
-        out_shape=[jax.ShapeDtypeStruct((NY, NZ), jnp.float32)] * FAR,
+        functools.partial(inverse_kernel, first),
+        out_shape=[jax.ShapeDtypeStruct((NY, NZ), jnp.float32)] * count,
         in_specs=specs(7),
-        out_specs=specs(FAR),
+        out_specs=specs(count),
         compiler_params=params(),
         cost_estimate=cost(),
         name="inverse_planes",
     )(potential, *bands, right, left)
 
 
-def solve(spectrum, squares, base, ahead, back):
+def solve(spectrum, squares, lanes, ahead, back):
     return pl.pallas_call(
         solve_kernel,
         out_shape=jax.ShapeDtypeStruct(spectrum.shape, jnp.float32),
@@ -176,7 +194,7 @@
         compiler_params=params(),
         cost_estimate=cost(),
         name="solve_columns",
-    )(spectrum, squares, base, ahead, back)
+    )(spectrum, squares, lanes, ahead, back)
 
 
 def exchange(value):
@@ -189,7 +207,9 @@
 
 def local(orbitals, trials, owner_group, block_index):
     plane_table = basis(NY)
-    column_table = basis(NX)
+    column_table = np.einsum(
+        "ab,kps->aksbp", np.eye(2), basis(NX).reshape(NX, FAR, SHARE)
+    ).reshape(2 * NX, 2 * NX)
     right_ahead = jnp.asarray(right_table(plane_table.T))
     left_ahead = jnp.asarray(left_table(plane_table))
     right_back = jnp.asarray(right_table(plane_table))
@@ -197,10 +217,7 @@
     column_ahead = jnp.asarray(left_table(column_table))
     column_back = jnp.asarray(left_table(column_table.T))
     squares = np.broadcast_to((frequencies(NX)[:, None] ** 2), (NX, NZ)).astype(np.float32)
-    grid_squares = 1 + frequencies(NY)[:, None] ** 2 + frequencies(NZ)[None, :] ** 2
-    base = lax.dynamic_slice_in_dim(
-        jnp.asarray(grid_squares.astype(np.float32)), lax.axis_index(SPREAD) * ROWS, ROWS, 0
-    )
+    lanes = (frequencies(NZ)[None, :] ** 2).astype(np.float32)
 
     group = lax.axis_index(("yl", "c"))
     mine = jnp.sum(jnp.where(owner_group == group, block_index, 0)) * BLOCK
@@ -224,15 +241,14 @@
     across, trial_planes = lax.optimization_barrier((across, trial_planes))
     bands = (own, swap(own, "c"), across, swap(across, "c"))
     spectrum = forward([trial] + trial_planes, bands, right_ahead, left_ahead)
-    spectrum, base = lax.optimization_barrier((spectrum, base))
     spectrum = solve(
-        exchange(spectrum), jnp.asarray(squares), base, column_ahead, column_back
-    )
-    planes = inverse(exchange(spectrum), bands, right_back, left_back)
-    total = planes[0]
-    for plane, perm in zip(planes[1:], back):
-        total = total + lax.ppermute(plane, "zh", perm)
-    return total[None, None]
+        exchange(spectrum), jnp.asarray(squares), jnp.asarray(lanes), column_ahead, column_back
+    )
+    potential = exchange(spectrum)
+    planes = inverse(1, FAR - 1, potential, bands, right_back, left_back)
+    planes = [lax.ppermute(plane, "zh", perm) for plane, perm in zip(planes, back)]
+    total = inverse(0, 1, potential, bands, right_back, left_back)[0]
+    return sum(planes, total)[None, None]
 
 
 def solution(mesh):

time: 127 us -> 126 us (level)
  transfers between devices with their start and end apart: 12 -> 12, of which waited for: 8 -> 8; matrix products, arithmetic and copies ran while one was open for 1% -> 0% of each run, Pallas kernels for 0% -> 0%
where the time goes in v2:
time: 126 us
  blocking collectives  68.7 us (55%)
  starting transfers between devices  25.7 us (20%)
  waiting for transfers between devices  21.4 us (17%)
  Pallas kernels  6.37 us (5%)
  other arithmetic  2.04 us (2%)
    all_to_all x2, blocking collectives, exchange(): return lax.all_to_all(value, SPREAD, 0, 0, tiled=True)  68.7 us
    ppermute x3, starting transfers between devices, local(): lax.ppermute(bands_for(far - step), 'zh', there[step - 1])  10.2 us
    ppermute x3, waiting for transfers between devices, local(): lax.ppermute(bands_for(far - step), 'zh', there[step - 1])  9.39 us
    ppermute x3, starting transfers between devices, local(): trial_planes = [lax.ppermute(trial, 'zh', perm) for perm in there]  7.74 us
    ppermute x3, starting transfers between devices, local(): lax.ppermute(plane, 'zh', perm)  6.07 us
    ppermute x3, waiting for transfers between devices, local(): lax.ppermute(plane, 'zh', perm)  5.37 us
    ppermute x3, waiting for transfers between devices, local(): trial_planes = [lax.ppermute(trial, 'zh', perm) for perm in there]  4.76 us
    pallas_call x1, Pallas kernels, solve(): pl.pallas_call(solve_kernel, out_shape=jax.ShapeDtypeStruct(spectrum.shap...  3.22 us
  transfers between devices with their start and end apart: 12, of which 8 were waited for; matrix products, arithmetic and copies ran while one was open for 0% of the time, Pallas kernels for 0%

profile of v2, /device:TPU:2, one launch (start us, length us, event | category | flops | bytes accessed | tf_op | source)
XLA Modules:
  0.0 126.3 jit_solution(1964605632224810504)
XLA Ops:
  0.0 0.0 copy-start.4
  0.0 0.0 copy-start.5
  0.0 0.0 copy-start.6
  0.0 1.4 %fusion = s32[]{:T(128)} fusion(s32[4]{0:T(128)} %param.15, s32[4]{0:T(128)} %param.14, s32[]{:T(128)S(6)} %add.57), kind=kLoop, calls=%fused_computation.7 | loop fusion | flops 11 | bytes 40 | tf_op jit(solution)/shard_map/reduce_sum | solution.py:223
  2.1 1.1 dynamic-slice_bitcast_fusion.3
  3.2 6.4 %collective-permute-start = (f32[2,128,128]{2,1,0:T(8,128)S(1)}, f32[2,128,128]{2,1,0:T(8,128)S(1)}, u32[]{:S(2)}, u32[]{:S(2)}) collective-permute-start(f32[2,128,128]{2,1,0:T(8,128)S(1)} %get-tuple-element.24), channel_id=1, source_target_pairs={{0,48},{16,0},{32,16},{48,32},{1,49},{17,1},{33,17},{49,33},{2,50}... | collective-permute-start | bytes 393224 | tf_op jit(solution)/shard_map/ppermute | solution.py:236
  9.6 0.0 collective-permute-start.2
  9.6 3.8 %collective-permute-start.1 = (f32[2,128,128]{2,1,0:T(8,128)S(1)}, f32[2,128,128]{2,1,0:T(8,128)S(1)}, u32[]{:S(2)}, u32[]{:S(2)}) collective-permute-start(f32[2,128,128]{2,1,0:T(8,128)S(1)} %get-tuple-element.26), channel_id=1, source_target_pairs={{0,32},{16,48},{32,0},{48,16},{1,33},{17,49},{33,1},{49,17},{2,34}... | collective-permute-start | bytes 393224 | tf_op jit(solution)/shard_map/ppermute | solution.py:236
  13.4 6.8 %collective-permute-done = f32[2,128,128]{2,1,0:T(8,128)S(1)} collective-permute-done((f32[2,128,128]{2,1,0:T(8,128)S(1)}, f32[2,128,128]{2,1,0:T(8,128)S(1)}, u32[]{:S(2)}, u32[]{:S(2)}) %collective-permute-start) | collective-permute-done | bytes 131104 | tf_op jit(solution)/shard_map/ppermute | solution.py:236
  20.2 2.6 %collective-permute-done.2 = f32[2,128,128]{2,1,0:T(8,128)S(1)} collective-permute-done((f32[2,128,128]{2,1,0:T(8,128)S(1)}, f32[2,128,128]{2,1,0:T(8,128)S(1)}, u32[]{:S(2)}, u32[]{:S(2)}) %collective-permute-start.2) | collective-permute-done | bytes 131104 | tf_op jit(solution)/shard_map/ppermute | solution.py:236
  22.8 0.0 collective-permute-done.1
  22.8 1.7 %collective-permute-start.3 = (f32[4,2,128,128]{3,2,1,0:T(8,128)S(1)}, f32[4,2,128,128]{3,2,1,0:T(8,128)S(1)}, u32[]{:S(2)}, u32[]{:S(2)}) collective-permute-start(f32[4,2,128,128]{3,2,1,0:T(8,128)S(1)} %pad_maximum_fusion.refs_4_.own), channel_id=1, source_target_pairs={{0,128},{128,0},{1,129},{129,1},{2,130},{130,2},{3,131},{131,3},{4... | collective-permute-start | bytes 1572872 | tf_op jit(solution)/shard_map/ppermute | solution.py:205
  24.5 0.0 copy-done.6
  24.5 4.2 %collective-permute-start.6 = (f32[1,128,128]{2,1,0:T(8,128)S(1)}, f32[1,128,128]{2,1,0:T(8,128)S(1)}, u32[]{:S(2)}, u32[]{:S(2)}) collective-permute-start(f32[1,128,128]{2,1,0:T(8,128)S(1)} %bitcast.14), channel_id=1, source_target_pairs={{0,16},{16,32},{32,48},{48,0},{1,17},{17,33},{33,49},{49,1},{2,18}... | collective-permute-start | bytes 196616 | tf_op jit(solution)/shard_map/ppermute | solution.py:240
  28.7 2.1 %collective-permute-start.5 = (f32[1,128,128]{2,1,0:T(8,128)S(1)}, f32[1,128,128]{2,1,0:T(8,128)S(1)}, u32[]{:S(2)}, u32[]{:S(2)}) collective-permute-start(f32[1,128,128]{2,1,0:T(8,128)S(1)} %bitcast.15), channel_id=1, source_target_pairs={{0,32},{16,48},{32,0},{48,16},{1,33},{17,49},{33,1},{49,17},{2,34}... | collective-permute-start | bytes 196616 | tf_op jit(solution)/shard_map/ppermute | solution.py:240
  30.8 1.5 %collective-permute-start.4 = (f32[1,128,128]{2,1,0:T(8,128)S(1)}, f32[1,128,128]{2,1,0:T(8,128)S(1)}, u32[]{:S(2)}, u32[]{:S(2)}) collective-permute-start(f32[1,128,128]{2,1,0:T(8,128)S(1)} %bitcast.16), channel_id=1, source_target_pairs={{0,48},{16,0},{32,16},{48,32},{1,49},{17,1},{33,17},{49,33},{2,50}... | collective-permute-start | bytes 196616 | tf_op jit(solution)/shard_map/ppermute | solution.py:240
  32.2 0.0 collective-permute-start.7
  32.3 0.0 collective-permute-done.6.refs_3_
  32.3 4.7 %collective-permute-done.5.refs_2_ = f32[1,128,128]{2,1,0:T(8,128)S(1)} collective-permute-done((f32[1,128,128]{2,1,0:T(8,128)S(1)}, f32[1,128,128]{2,1,0:T(8,128)S(1)}, u32[]{:S(2)}, u32[]{:S(2)}) %collective-permute-start.5) | collective-permute-done | bytes 65568 | tf_op jit(solution)/shard_map/ppermute | solution.py:240
  37.0 0.1 collective-permute-done.4.refs_1_
  37.0 0.0 collective-permute-done.3.refs_6_.third
  37.0 0.0 collective-permute-start.8
  37.0 0.0 collective-permute-done.7.refs_5_.second
  37.0 1.9 %collective-permute-done.8.refs_7_.fourth = f32[4,2,128,128]{3,2,1,0:T(8,128)S(1)} collective-permute-done((f32[4,2,128,128]{3,2,1,0:T(8,128)S(1)}, f32[4,2,128,128]{3,2,1,0:T(8,128)S(1)}, u32[]{:S(2)}, u32[]{:S(2)}) %collective-permute-start.8) | collective-permute-done | bytes 524320 | tf_op jit(solution)/shard_map/ppermute | solution.py:205
  38.9 0.0 copy-done.4
  38.9 0.0 copy-done.5
  38.9 1.4 %forward_planes.1 = f32[16,32,8,128]{3,2,1,0:T(8,128)S(1)} custom-call(f32[1,128,128]{2,1,0:T(8,128)S(1)} %bitcast.17, f32[1,128,128]{2,1,0:T(8,128)S(1)} %collective-permute-done.4.refs_1_, f32[1,128,128]{2,1,0:T(8,128)S(1)} %collective-permute-done.5.refs_2_, f32[1,128,128]{2,1,0:T(8,128)S(1)} %collective-permute-done.6.refs_3_, ...), custom_call_target="tpu_custom_call" | custom-call | flops 805306368 | bytes 4194304 | tf_op jit(solution)/shard_map/forward_planes/pallas_call | solution.py:165
  40.4 0.0 copy-start.2
  40.4 0.0 copy-start.3
  40.4 0.0 copy-start.7
  40.4 0.0 copy-start.8
  40.4 36.1 %all_to_all.10.spectrum = f32[16,32,8,128]{3,2,1,0:T(8,128)S(1)} all-to-all(f32[16,32,8,128]{3,2,1,0:T(8,128)S(1)} %forward_planes.1), channel_id=1, replica_groups=mesh['yl'=2,'c'=2,'zh'=4,'z0'=2,'x'=4,'yh'=2] {'z0','x','yh'}, dimensions={0} | all-to-all | bytes 4194304 | tf_op jit(solution)/shard_map/all_to_all | solution.py:201
  76.5 0.0 copy-done.2
  76.5 0.0 copy-done.3
  76.5 0.0 copy-done.7
  76.5 0.0 copy-done.8
  76.5 3.2 %solve_columns.1 = f32[16,32,8,128]{3,2,1,0:T(8,128)S(1)} custom-call(f32[16,32,8,128]{3,2,1,0:T(8,128)S(1)} %all_to_all.10.spectrum, f32[64,128]{1,0:T(8,128)S(1)} %copy-done.7, f32[1,128]{1,0:T(1,128)S(1)} %copy-done.8, bf16[256,256]{1,0:T(8,128)(2,1)S(1)} %copy-done.3, bf16[256,256]{1,0:T(8,128)(2,1)S(1)} %copy-done.2), custom_call_target="tpu_custom_call" | custom-call | flops 805306368 | bytes 4194304 | tf_op jit(solution)/shard_map/solve_columns/pallas_call | solution.py:189
  79.8 0.0 copy-start
  79.8 0.0 copy-start.1
  79.8 32.7 %all_to_all.11.potential = f32[16,32,8,128]{3,2,1,0:T(8,128)S(1)} all-to-all(f32[16,32,8,128]{3,2,1,0:T(8,128)S(1)} %solve_columns.1), channel_id=1, replica_groups=mesh['yl'=2,'c'=2,'zh'=4,'z0'=2,'x'=4,'yh'=2] {'z0','x','yh'}, dimensions={0} | all-to-all | bytes 4194304 | tf_op jit(solution)/shard_map/all_to_all | solution.py:201
  112.4 0.0 copy-done
  112.5 0.0 copy-done.1
  112.5 1.1 inverse_planes.3
  113.6 2.4 %collective-permute-start.9 = (f32[128,128]{1,0:T(8,128)S(1)}, f32[128,128]{1,0:T(8,128)S(1)}, u32[]{:S(2)}, u32[]{:S(2)}) collective-permute-start(f32[128,128]{1,0:T(8,128)S(1)} %get-tuple-element.20), channel_id=1, source_target_pairs={{0,16},{16,32},{32,48},{48,0},{1,17},{17,33},{33,49},{49,1},{2,18}... | collective-permute-start | bytes 196616 | tf_op jit(solution)/shard_map/ppermute | solution.py:249
  116.0 2.9 %collective-permute-start.10 = (f32[128,128]{1,0:T(8,128)S(1)}, f32[128,128]{1,0:T(8,128)S(1)}, u32[]{:S(2)}, u32[]{:S(2)}) collective-permute-start(f32[128,128]{1,0:T(8,128)S(1)} %get-tuple-element.21), channel_id=1, source_target_pairs={{0,32},{16,48},{32,0},{48,16},{1,33},{17,49},{33,1},{49,17},{2,34}... | collective-permute-start | bytes 196616 | tf_op jit(solution)/shard_map/ppermute | solution.py:249
  118.9 0.8 collective-permute-start.11
  119.7 0.6 inverse_planes.2
  120.3 1.1 collective-permute-done.9
  121.3 2.8 %collective-permute-done.10 = f32[128,128]{1,0:T(8,128)S(1)} collective-permute-done((f32[128,128]{1,0:T(8,128)S(1)}, f32[128,128]{1,0:T(8,128)S(1)}, u32[]{:S(2)}, u32[]{:S(2)}) %collective-permute-start.10) | collective-permute-done | bytes 65568 | tf_op jit(solution)/shard_map/ppermute | solution.py:249
  124.2 1.5 %collective-permute-done.11 = f32[128,128]{1,0:T(8,128)S(1)} collective-permute-done((f32[128,128]{1,0:T(8,128)S(1)}, f32[128,128]{1,0:T(8,128)S(1)}, u32[]{:S(2)}, u32[]{:S(2)}) %collective-permute-start.11) | collective-permute-done | bytes 65568 | tf_op jit(solution)/shard_map/ppermute | solution.py:249
  125.6 0.6 add_bitcast_fusion
  (1 shorter events, 0.0 us)
Async XLA Ops:
  0.0 38.9 %copy-start.4 = (bf16[256,256]{1,0:T(8,128)(2,1)S(1)}, bf16[256,256]{1,0:T(8,128)(2,1)}, u32[]{:S(2)}) copy-start(bf16[256,256]{1,0:T(8,128)(2,1)} %constant.65.clone.refs_9_) | copy-start | bytes 393220
  0.0 38.9 %copy-start.5 = (bf16[256,256]{1,0:T(8,128)(2,1)S(1)}, bf16[256,256]{1,0:T(8,128)(2,1)}, u32[]{:S(2)}) copy-start(bf16[256,256]{1,0:T(8,128)(2,1)} %constant.64.clone.refs_8_) | copy-start | bytes 393220
  0.0 24.5 %copy-start.6 = (f32[1,1,128,128]{3,2,1,0:T(8,128)S(1)}, f32[1,1,128,128]{3,2,1,0:T(8,128)}, u32[]{:S(2)}) copy-start(f32[1,1,128,128]{3,2,1,0:T(8,128)} %param.13) | copy-start | bytes 196612
  3.2 17.0 %collective-permute-start = (f32[2,128,128]{2,1,0:T(8,128)S(1)}, f32[2,128,128]{2,1,0:T(8,128)S(1)}, u32[]{:S(2)}, u32[]{:S(2)}) collective-permute-start(f32[2,128,128]{2,1,0:T(8,128)S(1)} %get-tuple-element.24), channel_id=1, source_target_pairs={{0,48},{16,0},{32,16},{48,32},{1,49},{17,1},{33,17},{49,33},{2,50}... | collective-permute-start | bytes 393224 | tf_op jit(solution)/shard_map/ppermute | solution.py:236
  9.6 13.2 %collective-permute-start.2 = (f32[2,128,128]{2,1,0:T(8,128)S(1)}, f32[2,128,128]{2,1,0:T(8,128)S(1)}, u32[]{:S(2)}, u32[]{:S(2)}) collective-permute-start(f32[2,128,128]{2,1,0:T(8,128)S(1)} %get-tuple-element.25), channel_id=1, source_target_pairs={{0,16},{16,32},{32,48},{48,0},{1,17},{17,33},{33,49},{49,1},{2,18}... | collective-permute-start | bytes 393224 | tf_op jit(solution)/shard_map/ppermute | solution.py:236
  9.6 13.2 %collective-permute-start.1 = (f32[2,128,128]{2,1,0:T(8,128)S(1)}, f32[2,128,128]{2,1,0:T(8,128)S(1)}, u32[]{:S(2)}, u32[]{:S(2)}) collective-permute-start(f32[2,128,128]{2,1,0:T(8,128)S(1)} %get-tuple-element.26), channel_id=1, source_target_pairs={{0,32},{16,48},{32,0},{48,16},{1,33},{17,49},{33,1},{49,17},{2,34}... | collective-permute-start | bytes 393224 | tf_op jit(solution)/shard_map/ppermute | solution.py:236
  22.8 14.2 %collective-permute-start.3 = (f32[4,2,128,128]{3,2,1,0:T(8,128)S(1)}, f32[4,2,128,128]{3,2,1,0:T(8,128)S(1)}, u32[]{:S(2)}, u32[]{:S(2)}) collective-permute-start(f32[4,2,128,128]{3,2,1,0:T(8,128)S(1)} %pad_maximum_fusion.refs_4_.own), channel_id=1, source_target_pairs={{0,128},{128,0},{1,129},{129,1},{2,130},{130,2},{3,131},{131,3},{4... | collective-permute-start | bytes 1572872 | tf_op jit(solution)/shard_map/ppermute | solution.py:205
  24.5 7.7 %collective-permute-start.6 = (f32[1,128,128]{2,1,0:T(8,128)S(1)}, f32[1,128,128]{2,1,0:T(8,128)S(1)}, u32[]{:S(2)}, u32[]{:S(2)}) collective-permute-start(f32[1,128,128]{2,1,0:T(8,128)S(1)} %bitcast.14), channel_id=1, source_target_pairs={{0,16},{16,32},{32,48},{48,0},{1,17},{17,33},{33,49},{49,1},{2,18}... | collective-permute-start | bytes 196616 | tf_op jit(solution)/shard_map/ppermute | solution.py:240
  28.7 8.3 %collective-permute-start.5 = (f32[1,128,128]{2,1,0:T(8,128)S(1)}, f32[1,128,128]{2,1,0:T(8,128)S(1)}, u32[]{:S(2)}, u32[]{:S(2)}) collective-permute-start(f32[1,128,128]{2,1,0:T(8,128)S(1)} %bitcast.15), channel_id=1, source_target_pairs={{0,32},{16,48},{32,0},{48,16},{1,33},{17,49},{33,1},{49,17},{2,34}... | collective-permute-start | bytes 196616 | tf_op jit(solution)/shard_map/ppermute | solution.py:240
  30.8 6.2 %collective-permute-start.4 = (f32[1,128,128]{2,1,0:T(8,128)S(1)}, f32[1,128,128]{2,1,0:T(8,128)S(1)}, u32[]{:S(2)}, u32[]{:S(2)}) collective-permute-start(f32[1,128,128]{2,1,0:T(8,128)S(1)} %bitcast.16), channel_id=1, source_target_pairs={{0,48},{16,0},{32,16},{48,32},{1,49},{17,1},{33,17},{49,33},{2,50}... | collective-permute-start | bytes 196616 | tf_op jit(solution)/shard_map/ppermute | solution.py:240
  32.2 4.8 %collective-permute-start.7 = (f32[4,2,128,128]{3,2,1,0:T(8,128)S(1)}, f32[4,2,128,128]{3,2,1,0:T(8,128)S(1)}, u32[]{:S(2)}, u32[]{:S(2)}) collective-permute-start(f32[4,2,128,128]{3,2,1,0:T(8,128)S(1)} %pad_maximum_fusion.refs_4_.own), channel_id=1, source_target_pairs={{0,64},{64,0},{1,65},{65,1},{2,66},{66,2},{3,67},{67,3},{4,68},{68... | collective-permute-start | bytes 1572872 | tf_op jit(solution)/shard_map/ppermute | solution.py:205
  37.0 1.9 %collective-permute-start.8 = (f32[4,2,128,128]{3,2,1,0:T(8,128)S(1)}, f32[4,2,128,128]{3,2,1,0:T(8,128)S(1)}, u32[]{:S(2)}, u32[]{:S(2)}) collective-permute-start(f32[4,2,128,128]{3,2,1,0:T(8,128)S(1)} %collective-permute-done.3.refs_6_.third), channel_id=1, source_target_pairs={{0,64},{64,0},{1,65},{65,1},{2,66},{66,2},{3,67},{67,3},{4,68},{68... | collective-permute-start | bytes 1572872 | tf_op jit(solution)/shard_map/ppermute | solution.py:205
  40.4 36.1 %copy-start.2 = (bf16[256,256]{1,0:T(8,128)(2,1)S(1)}, bf16[256,256]{1,0:T(8,128)(2,1)}, u32[]{:S(2)}) copy-start(bf16[256,256]{1,0:T(8,128)(2,1)} %constant.69.clone.back) | copy-start | bytes 393220
  40.4 36.1 %copy-start.3 = (bf16[256,256]{1,0:T(8,128)(2,1)S(1)}, bf16[256,256]{1,0:T(8,128)(2,1)}, u32[]{:S(2)}) copy-start(bf16[256,256]{1,0:T(8,128)(2,1)} %constant.68.clone.ahead) | copy-start | bytes 393220
  40.4 36.1 %copy-start.7 = (f32[64,128]{1,0:T(8,128)S(1)}, f32[64,128]{1,0:T(8,128)}, u32[]{:S(2)}) copy-start(f32[64,128]{1,0:T(8,128)} %constant.70.clone.squares) | copy-start | bytes 98308
  40.4 36.1 %copy-start.8 = (f32[1,128]{1,0:T(1,128)S(1)}, f32[1,128]{1,0:T(1,128)}, u32[]{:S(2)}) copy-start(f32[1,128]{1,0:T(1,128)} %constant.71.clone.lanes) | copy-start | bytes 1540
  79.8 32.7 %copy-start = (bf16[256,256]{1,0:T(8,128)(2,1)S(1)}, bf16[256,256]{1,0:T(8,128)(2,1)}, u32[]{:S(2)}) copy-start(bf16[256,256]{1,0:T(8,128)(2,1)} %constant.67.clone.left) | copy-start | bytes 393220
  79.8 32.7 %copy-start.1 = (bf16[256,256]{1,0:T(8,128)(2,1)S(1)}, bf16[256,256]{1,0:T(8,128)(2,1)}, u32[]{:S(2)}) copy-start(bf16[256,256]{1,0:T(8,128)(2,1)} %constant.66.clone.right) | copy-start | bytes 393220
  113.6 7.7 %collective-permute-start.9 = (f32[128,128]{1,0:T(8,128)S(1)}, f32[128,128]{1,0:T(8,128)S(1)}, u32[]{:S(2)}, u32[]{:S(2)}) collective-permute-start(f32[128,128]{1,0:T(8,128)S(1)} %get-tuple-element.20), channel_id=1, source_target_pairs={{0,16},{16,32},{32,48},{48,0},{1,17},{17,33},{33,49},{49,1},{2,18}... | collective-permute-start | bytes 196616 | tf_op jit(solution)/shard_map/ppermute | solution.py:249
  116.0 8.2 %collective-permute-start.10 = (f32[128,128]{1,0:T(8,128)S(1)}, f32[128,128]{1,0:T(8,128)S(1)}, u32[]{:S(2)}, u32[]{:S(2)}) collective-permute-start(f32[128,128]{1,0:T(8,128)S(1)} %get-tuple-element.21), channel_id=1, source_target_pairs={{0,32},{16,48},{32,0},{48,16},{1,33},{17,49},{33,1},{49,17},{2,34}... | collective-permute-start | bytes 196616 | tf_op jit(solution)/shard_map/ppermute | solution.py:249
  118.9 6.8 %collective-permute-start.11 = (f32[128,128]{1,0:T(8,128)S(1)}, f32[128,128]{1,0:T(8,128)S(1)}, u32[]{:S(2)}, u32[]{:S(2)}) collective-permute-start(f32[128,128]{1,0:T(8,128)S(1)} %get-tuple-element.22), channel_id=1, source_target_pairs={{0,48},{16,0},{32,16},{48,32},{1,49},{17,1},{33,17},{49,33},{2,50}... | collective-permute-start | bytes 196616 | tf_op jit(solution)/shard_map/ppermute | solution.py:249

commit v3 on v2

--- a/solution.py
+++ b/solution.py
@@ -14,7 +14,7 @@
 NX, NY, NZ = 64, 128, 128
 AXES = ("yl", "c", "zh", "z0", "x", "yh")
 SIZES = (2, 2, 4, 2, 4, 2)
-SPREAD = ("z0", "x", "yh")
+SPREAD = ("yh", "x", "z0")
 FAR = 4
 SHARE = 16
 ROWS = NY // SHARE
@@ -115,7 +115,7 @@
 
 
 def solve_kernel(spectrum, squares, lanes, ahead, back, out):
-    first = (lax.axis_index("z0") * 8 + lax.axis_index("x") * 2 + lax.axis_index("yh")) * ROWS
+    first = (lax.axis_index("yh") * 8 + lax.axis_index("x") * 2 + lax.axis_index("z0") * 1) * ROWS
     for pair in range(0, ROWS, 2):
         kernels = []
         for row in (pair, pair + 1):
@@ -207,8 +207,9 @@
 
 def local(orbitals, trials, owner_group, block_index):
     plane_table = basis(NY)
+    by_device = basis(NX).reshape(NX, FAR, 2, 4, 2).transpose(0, 1, 4, 3, 2).reshape(NX, FAR, SHARE)
     column_table = np.einsum(
-        "ab,kps->aksbp", np.eye(2), basis(NX).reshape(NX, FAR, SHARE)
+        "ab,kps->aksbp", np.eye(2), by_device
     ).reshape(2 * NX, 2 * NX)
     right_ahead = jnp.asarray(right_table(plane_table.T))
     left_ahead = jnp.asarray(left_table(plane_table))
@@ -223,7 +224,7 @@
     mine = jnp.sum(jnp.where(owner_group == group, block_index, 0)) * BLOCK
     far = lax.axis_index("zh")
 
-    def bands_for(place):
+    def bands_for(place, mine):
         start = mine + lax.rem(place + FAR, FAR) * KEEP
         return lax.dynamic_slice_in_dim(orbitals[:, 0], start, KEEP, 0)
 
@@ -231,9 +232,15 @@
     steps = range(1, FAR)
     there = [[(i, (i - step) % FAR) for i in range(FAR)] for step in steps]
     back = [[(i, (i + step) % FAR) for i in range(FAR)] for step in steps]
+    middle = bands_for(far - 2, mine)
+    mine, middle = lax.optimization_barrier((mine, middle))
     own = jnp.stack(
-        [bands_for(far)]
-        + [lax.ppermute(bands_for(far - step), "zh", there[step - 1]) for step in steps]
+        [
+            bands_for(far, mine),
+            lax.ppermute(bands_for(far - 1, mine), "zh", there[0]),
+            lax.ppermute(middle, "zh", there[1]),
+            lax.ppermute(bands_for(far - 3, mine), "zh", there[2]),
+        ]
     )
     own, trial = lax.optimization_barrier((own, trial))
     across = swap(own, "yl")

time: 126 us -> 125 us (level); the launches traced: 126 us -> 123 us
  waiting for transfers between devices: 21.4 us -> 17.7 us
  starting transfers between devices: 25.7 us -> 29.2 us
  blocking collectives: 68.7 us -> 65.3 us
    all_to_all x2, blocking collectives: 68.7 us -> 65.3 us  [exchange(): return lax.all_to_all(value, SPREAD, 0, 0, tiled=True)]
    ppermute x3, starting transfers between devices: 6.07 us -> 8.99 us  [local(): lax.ppermute(plane, 'zh', perm)]
    ppermute x3, waiting for transfers between devices: 5.37 us -> 2.77 us  [local(): lax.ppermute(plane, 'zh', perm)]
    ppermute x3, waiting for transfers between devices: 9.39 us -> 7.25 us  [the longest x1 4.73 us: local(): lax.ppermute(bands_for(far - 3, mine), 'zh', there[2])]
    ppermute x3, starting transfers between devices: 10.2 us -> 11.5 us  [the longest x1 7.28 us: local(): lax.ppermute(middle, 'zh', there[1])]
  transfers between devices with their start and end apart: 12 -> 12, of which waited for: 8 -> 7; matrix products, arithmetic and copies ran while one was open for 0% -> 1% of each run, Pallas kernels for 0% -> 0%
where the time goes in v3:
time: 125 us; the launch traced here: 123 us
  blocking collectives  65.3 us (52%)
  starting transfers between devices  29.2 us (23%)
  waiting for transfers between devices  17.7 us (14%)
  Pallas kernels  6.34 us (5%)
  other arithmetic  2.05 us (2%)
  local copies, waits for them, and re-layouts  2.03 us (2%)
    all_to_all x2, blocking collectives, exchange(): return lax.all_to_all(value, SPREAD, 0, 0, tiled=True)  65.3 us
    ppermute x3, starting transfers between devices, local(): lax.ppermute(plane, 'zh', perm)  8.99 us
    ppermute x1, starting transfers between devices, local(): lax.ppermute(middle, 'zh', there[1])  7.28 us
    ppermute x3, starting transfers between devices, local(): trial_planes = [lax.ppermute(trial, 'zh', perm) for perm in there]  7.06 us
    ppermute x3, waiting for transfers between devices, local(): trial_planes = [lax.ppermute(trial, 'zh', perm) for perm in there]  5.75 us
    ppermute x1, waiting for transfers between devices, local(): lax.ppermute(bands_for(far - 3, mine), 'zh', there[2])  4.73 us
    pallas_call x1, Pallas kernels, solve(): pl.pallas_call(solve_kernel, out_shape=jax.ShapeDtypeStruct(spectrum.shap...  3.19 us
    ppermute x3, waiting for transfers between devices, local(): lax.ppermute(plane, 'zh', perm)  2.77 us
  transfers between devices with their start and end apart: 12, of which 7 were waited for; matrix products, arithmetic and copies ran while one was open for 1% of the time, Pallas kernels for 0%

profile of v3, /device:TPU:2, one launch (start us, length us, event | category | flops | bytes accessed | tf_op | source)
XLA Modules:
  0.0 123.4 jit_solution(6135989430347400734)
XLA Ops:
  0.0 0.0 copy-start.4
  0.0 0.0 copy-start.5
  0.0 0.0 copy-start.6
  0.0 1.4 %fusion = s32[]{:T(128)} fusion(s32[4]{0:T(128)} %param.15, s32[4]{0:T(128)} %param.14, s32[]{:T(128)S(6)} %add.57), kind=kLoop, calls=%fused_computation.7 | loop fusion | flops 11 | bytes 40 | tf_op jit(solution)/shard_map/reduce_sum | solution.py:224
  2.0 0.9 dynamic-slice_bitcast_fusion.3
  3.0 7.3 %collective-permute-start.1 = (f32[2,128,128]{2,1,0:T(8,128)S(1)}, f32[2,128,128]{2,1,0:T(8,128)S(1)}, u32[]{:S(2)}, u32[]{:S(2)}) collective-permute-start(f32[2,128,128]{2,1,0:T(8,128)S(1)} %dynamic-slice_bitcast_fusion.3), channel_id=1, source_target_pairs={{0,32},{16,48},{32,0},{48,16},{1,33},{17,49},{33,1},{49,17},{2,34}... | collective-permute-start | bytes 393224 | tf_op jit(solution)/shard_map/ppermute | solution.py:241
  10.2 1.1 dynamic-slice_bitcast_fusion.2
  11.3 1.6 %collective-permute-start.2 = (f32[2,128,128]{2,1,0:T(8,128)S(1)}, f32[2,128,128]{2,1,0:T(8,128)S(1)}, u32[]{:S(2)}, u32[]{:S(2)}) collective-permute-start(f32[2,128,128]{2,1,0:T(8,128)S(1)} %get-tuple-element.28), channel_id=1, source_target_pairs={{0,16},{16,32},{32,48},{48,0},{1,17},{17,33},{33,49},{49,1},{2,18}... | collective-permute-start | bytes 393224 | tf_op jit(solution)/shard_map/ppermute | solution.py:242
  12.9 2.7 %collective-permute-start = (f32[2,128,128]{2,1,0:T(8,128)S(1)}, f32[2,128,128]{2,1,0:T(8,128)S(1)}, u32[]{:S(2)}, u32[]{:S(2)}) collective-permute-start(f32[2,128,128]{2,1,0:T(8,128)S(1)} %get-tuple-element.29), channel_id=1, source_target_pairs={{0,48},{16,0},{32,16},{48,32},{1,49},{17,1},{33,17},{49,33},{2,50}... | collective-permute-start | bytes 393224 | tf_op jit(solution)/shard_map/ppermute | solution.py:240
  15.5 0.0 collective-permute-done.1
  15.6 4.7 %collective-permute-done.2 = f32[2,128,128]{2,1,0:T(8,128)S(1)} collective-permute-done((f32[2,128,128]{2,1,0:T(8,128)S(1)}, f32[2,128,128]{2,1,0:T(8,128)S(1)}, u32[]{:S(2)}, u32[]{:S(2)}) %collective-permute-start.2) | collective-permute-done | bytes 131104 | tf_op jit(solution)/shard_map/ppermute | solution.py:242
  20.3 2.5 %collective-permute-done = f32[2,128,128]{2,1,0:T(8,128)S(1)} collective-permute-done((f32[2,128,128]{2,1,0:T(8,128)S(1)}, f32[2,128,128]{2,1,0:T(8,128)S(1)}, u32[]{:S(2)}, u32[]{:S(2)}) %collective-permute-start) | collective-permute-done | bytes 131104 | tf_op jit(solution)/shard_map/ppermute | solution.py:240
  22.8 1.7 %collective-permute-start.3 = (f32[4,2,128,128]{3,2,1,0:T(8,128)S(1)}, f32[4,2,128,128]{3,2,1,0:T(8,128)S(1)}, u32[]{:S(2)}, u32[]{:S(2)}) collective-permute-start(f32[4,2,128,128]{3,2,1,0:T(8,128)S(1)} %pad_maximum_fusion.refs_4_.own), channel_id=1, source_target_pairs={{0,128},{128,0},{1,129},{129,1},{2,130},{130,2},{3,131},{131,3},{4... | collective-permute-start | bytes 1572872 | tf_op jit(solution)/shard_map/ppermute | solution.py:205
  24.5 0.0 copy-done.6
  24.5 1.4 %collective-permute-start.6 = (f32[1,128,128]{2,1,0:T(8,128)S(1)}, f32[1,128,128]{2,1,0:T(8,128)S(1)}, u32[]{:S(2)}, u32[]{:S(2)}) collective-permute-start(f32[1,128,128]{2,1,0:T(8,128)S(1)} %bitcast.14), channel_id=1, source_target_pairs={{0,16},{16,32},{32,48},{48,0},{1,17},{17,33},{33,49},{49,1},{2,18}... | collective-permute-start | bytes 196616 | tf_op jit(solution)/shard_map/ppermute | solution.py:247
  25.9 4.5 %collective-permute-start.5 = (f32[1,128,128]{2,1,0:T(8,128)S(1)}, f32[1,128,128]{2,1,0:T(8,128)S(1)}, u32[]{:S(2)}, u32[]{:S(2)}) collective-permute-start(f32[1,128,128]{2,1,0:T(8,128)S(1)} %bitcast.15), channel_id=1, source_target_pairs={{0,32},{16,48},{32,0},{48,16},{1,33},{17,49},{33,1},{49,17},{2,34}... | collective-permute-start | bytes 196616 | tf_op jit(solution)/shard_map/ppermute | solution.py:247
  30.4 1.1 collective-permute-start.4
  31.5 0.0 collective-permute-start.7
  31.5 0.0 collective-permute-done.6.refs_3_
  31.6 4.5 %collective-permute-done.5.refs_2_ = f32[1,128,128]{2,1,0:T(8,128)S(1)} collective-permute-done((f32[1,128,128]{2,1,0:T(8,128)S(1)}, f32[1,128,128]{2,1,0:T(8,128)S(1)}, u32[]{:S(2)}, u32[]{:S(2)}) %collective-permute-start.5) | collective-permute-done | bytes 65568 | tf_op jit(solution)/shard_map/ppermute | solution.py:247
  36.1 1.2 %collective-permute-done.4.refs_1_ = f32[1,128,128]{2,1,0:T(8,128)S(1)} collective-permute-done((f32[1,128,128]{2,1,0:T(8,128)S(1)}, f32[1,128,128]{2,1,0:T(8,128)S(1)}, u32[]{:S(2)}, u32[]{:S(2)}) %collective-permute-start.4) | collective-permute-done | bytes 65568 | tf_op jit(solution)/shard_map/ppermute | solution.py:247
  37.3 0.0 collective-permute-done.3.refs_6_.third
  37.3 0.0 collective-permute-start.8
  37.3 0.0 collective-permute-done.7.refs_5_.second
  37.3 1.9 %collective-permute-done.8.refs_7_.fourth = f32[4,2,128,128]{3,2,1,0:T(8,128)S(1)} collective-permute-done((f32[4,2,128,128]{3,2,1,0:T(8,128)S(1)}, f32[4,2,128,128]{3,2,1,0:T(8,128)S(1)}, u32[]{:S(2)}, u32[]{:S(2)}) %collective-permute-start.8) | collective-permute-done | bytes 524320 | tf_op jit(solution)/shard_map/ppermute | solution.py:205
  39.2 0.0 copy-done.4
  39.2 0.0 copy-done.5
  39.2 1.4 %forward_planes.1 = f32[16,32,8,128]{3,2,1,0:T(8,128)S(1)} custom-call(f32[1,128,128]{2,1,0:T(8,128)S(1)} %bitcast.17, f32[1,128,128]{2,1,0:T(8,128)S(1)} %collective-permute-done.4.refs_1_, f32[1,128,128]{2,1,0:T(8,128)S(1)} %collective-permute-done.5.refs_2_, f32[1,128,128]{2,1,0:T(8,128)S(1)} %collective-permute-done.6.refs_3_, ...), custom_call_target="tpu_custom_call" | custom-call | flops 805306368 | bytes 4194304 | tf_op jit(solution)/shard_map/forward_planes/pallas_call | solution.py:165
  40.7 0.0 copy-start.2
  40.7 0.0 copy-start.3
  40.7 0.0 copy-start.7
  40.7 0.0 copy-start.8
  40.7 33.4 %all_to_all.10.spectrum = f32[16,32,8,128]{3,2,1,0:T(8,128)S(1)} all-to-all(f32[16,32,8,128]{3,2,1,0:T(8,128)S(1)} %forward_planes.1), channel_id=1, replica_groups=mesh['yl'=2,'c'=2,'zh'=4,'z0'=2,'x'=4,'yh'=2] {'yh','x','z0'}, dimensions={0} | all-to-all | bytes 4194304 | tf_op jit(solution)/shard_map/all_to_all | solution.py:201
  74.2 0.0 copy-done.2
  74.2 0.0 copy-done.3
  74.2 0.0 copy-done.7
  74.2 0.0 copy-done.8
  74.2 3.2 %solve_columns.1 = f32[16,32,8,128]{3,2,1,0:T(8,128)S(1)} custom-call(f32[16,32,8,128]{3,2,1,0:T(8,128)S(1)} %all_to_all.10.spectrum, f32[64,128]{1,0:T(8,128)S(1)} %copy-done.7, f32[1,128]{1,0:T(1,128)S(1)} %copy-done.8, bf16[256,256]{1,0:T(8,128)(2,1)S(1)} %copy-done.3, bf16[256,256]{1,0:T(8,128)(2,1)S(1)} %copy-done.2), custom_call_target="tpu_custom_call" | custom-call | flops 805306368 | bytes 4194304 | tf_op jit(solution)/shard_map/solve_columns/pallas_call | solution.py:189
  77.4 0.0 copy-start
  77.4 0.0 copy-start.1
  77.4 31.9 %all_to_all.11.potential = f32[16,32,8,128]{3,2,1,0:T(8,128)S(1)} all-to-all(f32[16,32,8,128]{3,2,1,0:T(8,128)S(1)} %solve_columns.1), channel_id=1, replica_groups=mesh['yl'=2,'c'=2,'zh'=4,'z0'=2,'x'=4,'yh'=2] {'yh','x','z0'}, dimensions={0} | all-to-all | bytes 4194304 | tf_op jit(solution)/shard_map/all_to_all | solution.py:201
  109.3 0.0 copy-done
  109.3 0.0 copy-done.1
  109.3 1.1 inverse_planes.3
  110.4 3.0 %collective-permute-start.9 = (f32[128,128]{1,0:T(8,128)S(1)}, f32[128,128]{1,0:T(8,128)S(1)}, u32[]{:S(2)}, u32[]{:S(2)}) collective-permute-start(f32[128,128]{1,0:T(8,128)S(1)} %get-tuple-element.24), channel_id=1, source_target_pairs={{0,16},{16,32},{32,48},{48,0},{1,17},{17,33},{33,49},{49,1},{2,18}... | collective-permute-start | bytes 196616 | tf_op jit(solution)/shard_map/ppermute | solution.py:256
  113.4 3.3 %collective-permute-start.10 = (f32[128,128]{1,0:T(8,128)S(1)}, f32[128,128]{1,0:T(8,128)S(1)}, u32[]{:S(2)}, u32[]{:S(2)}) collective-permute-start(f32[128,128]{1,0:T(8,128)S(1)} %get-tuple-element.25), channel_id=1, source_target_pairs={{0,32},{16,48},{32,0},{48,16},{1,33},{17,49},{33,1},{49,17},{2,34}... | collective-permute-start | bytes 196616 | tf_op jit(solution)/shard_map/ppermute | solution.py:256
  116.7 2.7 %collective-permute-start.11 = (f32[128,128]{1,0:T(8,128)S(1)}, f32[128,128]{1,0:T(8,128)S(1)}, u32[]{:S(2)}, u32[]{:S(2)}) collective-permute-start(f32[128,128]{1,0:T(8,128)S(1)} %get-tuple-element.26), channel_id=1, source_target_pairs={{0,48},{16,0},{32,16},{48,32},{1,49},{17,1},{33,17},{49,33},{2,50}... | collective-permute-start | bytes 196616 | tf_op jit(solution)/shard_map/ppermute | solution.py:256
  119.4 0.6 inverse_planes.2
  120.0 0.0 collective-permute-done.9
  120.0 2.4 %collective-permute-done.10 = f32[128,128]{1,0:T(8,128)S(1)} collective-permute-done((f32[128,128]{1,0:T(8,128)S(1)}, f32[128,128]{1,0:T(8,128)S(1)}, u32[]{:S(2)}, u32[]{:S(2)}) %collective-permute-start.10) | collective-permute-done | bytes 65568 | tf_op jit(solution)/shard_map/ppermute | solution.py:256
  122.4 0.4 collective-permute-done.11
  122.8 0.6 add_bitcast_fusion
  (1 shorter events, 0.0 us)
Async XLA Ops:
  0.0 39.2 %copy-start.4 = (bf16[256,256]{1,0:T(8,128)(2,1)S(1)}, bf16[256,256]{1,0:T(8,128)(2,1)}, u32[]{:S(2)}) copy-start(bf16[256,256]{1,0:T(8,128)(2,1)} %constant.65.clone.refs_9_) | copy-start | bytes 393220
  0.0 39.2 %copy-start.5 = (bf16[256,256]{1,0:T(8,128)(2,1)S(1)}, bf16[256,256]{1,0:T(8,128)(2,1)}, u32[]{:S(2)}) copy-start(bf16[256,256]{1,0:T(8,128)(2,1)} %constant.64.clone.refs_8_) | copy-start | bytes 393220
  0.0 24.5 %copy-start.6 = (f32[1,1,128,128]{3,2,1,0:T(8,128)S(1)}, f32[1,1,128,128]{3,2,1,0:T(8,128)}, u32[]{:S(2)}) copy-start(f32[1,1,128,128]{3,2,1,0:T(8,128)} %param.13) | copy-start | bytes 196612
  3.0 12.6 %collective-permute-start.1 = (f32[2,128,128]{2,1,0:T(8,128)S(1)}, f32[2,128,128]{2,1,0:T(8,128)S(1)}, u32[]{:S(2)}, u32[]{:S(2)}) collective-permute-start(f32[2,128,128]{2,1,0:T(8,128)S(1)} %dynamic-slice_bitcast_fusion.3), channel_id=1, source_target_pairs={{0,32},{16,48},{32,0},{48,16},{1,33},{17,49},{33,1},{49,17},{2,34}... | collective-permute-start | bytes 393224 | tf_op jit(solution)/shard_map/ppermute | solution.py:241
  11.3 9.0 %collective-permute-start.2 = (f32[2,128,128]{2,1,0:T(8,128)S(1)}, f32[2,128,128]{2,1,0:T(8,128)S(1)}, u32[]{:S(2)}, u32[]{:S(2)}) collective-permute-start(f32[2,128,128]{2,1,0:T(8,128)S(1)} %get-tuple-element.28), channel_id=1, source_target_pairs={{0,16},{16,32},{32,48},{48,0},{1,17},{17,33},{33,49},{49,1},{2,18}... | collective-permute-start | bytes 393224 | tf_op jit(solution)/shard_map/ppermute | solution.py:242
  12.9 9.9 %collective-permute-start = (f32[2,128,128]{2,1,0:T(8,128)S(1)}, f32[2,128,128]{2,1,0:T(8,128)S(1)}, u32[]{:S(2)}, u32[]{:S(2)}) collective-permute-start(f32[2,128,128]{2,1,0:T(8,128)S(1)} %get-tuple-element.29), channel_id=1, source_target_pairs={{0,48},{16,0},{32,16},{48,32},{1,49},{17,1},{33,17},{49,33},{2,50}... | collective-permute-start | bytes 393224 | tf_op jit(solution)/shard_map/ppermute | solution.py:240
  22.8 14.5 %collective-permute-start.3 = (f32[4,2,128,128]{3,2,1,0:T(8,128)S(1)}, f32[4,2,128,128]{3,2,1,0:T(8,128)S(1)}, u32[]{:S(2)}, u32[]{:S(2)}) collective-permute-start(f32[4,2,128,128]{3,2,1,0:T(8,128)S(1)} %pad_maximum_fusion.refs_4_.own), channel_id=1, source_target_pairs={{0,128},{128,0},{1,129},{129,1},{2,130},{130,2},{3,131},{131,3},{4... | collective-permute-start | bytes 1572872 | tf_op jit(solution)/shard_map/ppermute | solution.py:205
  24.5 7.1 %collective-permute-start.6 = (f32[1,128,128]{2,1,0:T(8,128)S(1)}, f32[1,128,128]{2,1,0:T(8,128)S(1)}, u32[]{:S(2)}, u32[]{:S(2)}) collective-permute-start(f32[1,128,128]{2,1,0:T(8,128)S(1)} %bitcast.14), channel_id=1, source_target_pairs={{0,16},{16,32},{32,48},{48,0},{1,17},{17,33},{33,49},{49,1},{2,18}... | collective-permute-start | bytes 196616 | tf_op jit(solution)/shard_map/ppermute | solution.py:247
  25.9 10.2 %collective-permute-start.5 = (f32[1,128,128]{2,1,0:T(8,128)S(1)}, f32[1,128,128]{2,1,0:T(8,128)S(1)}, u32[]{:S(2)}, u32[]{:S(2)}) collective-permute-start(f32[1,128,128]{2,1,0:T(8,128)S(1)} %bitcast.15), channel_id=1, source_target_pairs={{0,32},{16,48},{32,0},{48,16},{1,33},{17,49},{33,1},{49,17},{2,34}... | collective-permute-start | bytes 196616 | tf_op jit(solution)/shard_map/ppermute | solution.py:247
  30.4 6.9 %collective-permute-start.4 = (f32[1,128,128]{2,1,0:T(8,128)S(1)}, f32[1,128,128]{2,1,0:T(8,128)S(1)}, u32[]{:S(2)}, u32[]{:S(2)}) collective-permute-start(f32[1,128,128]{2,1,0:T(8,128)S(1)} %bitcast.16), channel_id=1, source_target_pairs={{0,48},{16,0},{32,16},{48,32},{1,49},{17,1},{33,17},{49,33},{2,50}... | collective-permute-start | bytes 196616 | tf_op jit(solution)/shard_map/ppermute | solution.py:247
  31.5 5.8 %collective-permute-start.7 = (f32[4,2,128,128]{3,2,1,0:T(8,128)S(1)}, f32[4,2,128,128]{3,2,1,0:T(8,128)S(1)}, u32[]{:S(2)}, u32[]{:S(2)}) collective-permute-start(f32[4,2,128,128]{3,2,1,0:T(8,128)S(1)} %pad_maximum_fusion.refs_4_.own), channel_id=1, source_target_pairs={{0,64},{64,0},{1,65},{65,1},{2,66},{66,2},{3,67},{67,3},{4,68},{68... | collective-permute-start | bytes 1572872 | tf_op jit(solution)/shard_map/ppermute | solution.py:205
  37.3 1.9 %collective-permute-start.8 = (f32[4,2,128,128]{3,2,1,0:T(8,128)S(1)}, f32[4,2,128,128]{3,2,1,0:T(8,128)S(1)}, u32[]{:S(2)}, u32[]{:S(2)}) collective-permute-start(f32[4,2,128,128]{3,2,1,0:T(8,128)S(1)} %collective-permute-done.3.refs_6_.third), channel_id=1, source_target_pairs={{0,64},{64,0},{1,65},{65,1},{2,66},{66,2},{3,67},{67,3},{4,68},{68... | collective-permute-start | bytes 1572872 | tf_op jit(solution)/shard_map/ppermute | solution.py:205
  40.7 33.5 %copy-start.2 = (bf16[256,256]{1,0:T(8,128)(2,1)S(1)}, bf16[256,256]{1,0:T(8,128)(2,1)}, u32[]{:S(2)}) copy-start(bf16[256,256]{1,0:T(8,128)(2,1)} %constant.69.clone.back) | copy-start | bytes 393220
  40.7 33.5 %copy-start.3 = (bf16[256,256]{1,0:T(8,128)(2,1)S(1)}, bf16[256,256]{1,0:T(8,128)(2,1)}, u32[]{:S(2)}) copy-start(bf16[256,256]{1,0:T(8,128)(2,1)} %constant.68.clone.ahead) | copy-start | bytes 393220
  40.7 33.5 %copy-start.7 = (f32[64,128]{1,0:T(8,128)S(1)}, f32[64,128]{1,0:T(8,128)}, u32[]{:S(2)}) copy-start(f32[64,128]{1,0:T(8,128)} %constant.70.clone.squares) | copy-start | bytes 98308
  40.7 33.5 %copy-start.8 = (f32[1,128]{1,0:T(1,128)S(1)}, f32[1,128]{1,0:T(1,128)}, u32[]{:S(2)}) copy-start(f32[1,128]{1,0:T(1,128)} %constant.71.clone.lanes) | copy-start | bytes 1540
  77.4 31.9 %copy-start = (bf16[256,256]{1,0:T(8,128)(2,1)S(1)}, bf16[256,256]{1,0:T(8,128)(2,1)}, u32[]{:S(2)}) copy-start(bf16[256,256]{1,0:T(8,128)(2,1)} %constant.67.clone.left) | copy-start | bytes 393220
  77.4 31.9 %copy-start.1 = (bf16[256,256]{1,0:T(8,128)(2,1)S(1)}, bf16[256,256]{1,0:T(8,128)(2,1)}, u32[]{:S(2)}) copy-start(bf16[256,256]{1,0:T(8,128)(2,1)} %constant.66.clone.right) | copy-start | bytes 393220
  110.4 9.6 %collective-permute-start.9 = (f32[128,128]{1,0:T(8,128)S(1)}, f32[128,128]{1,0:T(8,128)S(1)}, u32[]{:S(2)}, u32[]{:S(2)}) collective-permute-start(f32[128,128]{1,0:T(8,128)S(1)} %get-tuple-element.24), channel_id=1, source_target_pairs={{0,16},{16,32},{32,48},{48,0},{1,17},{17,33},{33,49},{49,1},{2,18}... | collective-permute-start | bytes 196616 | tf_op jit(solution)/shard_map/ppermute | solution.py:256
  113.4 9.0 %collective-permute-start.10 = (f32[128,128]{1,0:T(8,128)S(1)}, f32[128,128]{1,0:T(8,128)S(1)}, u32[]{:S(2)}, u32[]{:S(2)}) collective-permute-start(f32[128,128]{1,0:T(8,128)S(1)} %get-tuple-element.25), channel_id=1, source_target_pairs={{0,32},{16,48},{32,0},{48,16},{1,33},{17,49},{33,1},{49,17},{2,34}... | collective-permute-start | bytes 196616 | tf_op jit(solution)/shard_map/ppermute | solution.py:256
  116.7 6.1 %collective-permute-start.11 = (f32[128,128]{1,0:T(8,128)S(1)}, f32[128,128]{1,0:T(8,128)S(1)}, u32[]{:S(2)}, u32[]{:S(2)}) collective-permute-start(f32[128,128]{1,0:T(8,128)S(1)} %get-tuple-element.26), channel_id=1, source_target_pairs={{0,48},{16,0},{32,16},{48,32},{1,49},{17,1},{33,17},{49,33},{2,50}... | collective-permute-start | bytes 196616 | tf_op jit(solution)/shard_map/ppermute | solution.py:256

commit v4 on v3

--- a/solution.py
+++ b/solution.py
@@ -14,7 +14,7 @@
 NX, NY, NZ = 64, 128, 128
 AXES = ("yl", "c", "zh", "z0", "x", "yh")
 SIZES = (2, 2, 4, 2, 4, 2)
-SPREAD = ("yh", "x", "z0")
+SPREAD = ("x", "yh", "z0")
 FAR = 4
 SHARE = 16
 ROWS = NY // SHARE
@@ -115,7 +115,7 @@
 
 
 def solve_kernel(spectrum, squares, lanes, ahead, back, out):
-    first = (lax.axis_index("yh") * 8 + lax.axis_index("x") * 2 + lax.axis_index("z0") * 1) * ROWS
+    first = (lax.axis_index("x") * 4 + lax.axis_index("yh") * 2 + lax.axis_index("z0") * 1) * ROWS
     for pair in range(0, ROWS, 2):
         kernels = []
         for row in (pair, pair + 1):
@@ -207,7 +207,7 @@
 
 def local(orbitals, trials, owner_group, block_index):
     plane_table = basis(NY)
-    by_device = basis(NX).reshape(NX, FAR, 2, 4, 2).transpose(0, 1, 4, 3, 2).reshape(NX, FAR, SHARE)
+    by_device = basis(NX).reshape(NX, FAR, 2, 4, 2).transpose(0, 1, 3, 4, 2).reshape(NX, FAR, SHARE)
     column_table = np.einsum(
         "ab,kps->aksbp", np.eye(2), by_device
     ).reshape(2 * NX, 2 * NX)

time: 125 us -> 125 us (level)
  no operation moved by 1% of the time
where the time goes in v4:
time: 125 us; the launch traced here: 124 us
  blocking collectives  65.9 us (53%)
  starting transfers between devices  29.2 us (23%)
  waiting for transfers between devices  17.6 us (14%)
  Pallas kernels  6.35 us (5%)
  other arithmetic  2.05 us (2%)
  local copies, waits for them, and re-layouts  2.03 us (2%)
    all_to_all x2, blocking collectives, exchange(): return lax.all_to_all(value, SPREAD, 0, 0, tiled=True)  65.9 us
    ppermute x3, starting transfers between devices, local(): lax.ppermute(plane, 'zh', perm)  9.01 us
    ppermute x1, starting transfers between devices, local(): lax.ppermute(middle, 'zh', there[1])  7.28 us
    ppermute x3, starting transfers between devices, local(): trial_planes = [lax.ppermute(trial, 'zh', perm) for perm in there]  7.06 us
    ppermute x3, waiting for transfers between devices, local(): trial_planes = [lax.ppermute(trial, 'zh', perm) for perm in there]  5.75 us
    ppermute x1, waiting for transfers between devices, local(): lax.ppermute(bands_for(far - 3, mine), 'zh', there[2])  4.73 us
    pallas_call x1, Pallas kernels, solve(): pl.pallas_call(solve_kernel, out_shape=jax.ShapeDtypeStruct(spectrum.shap...  3.19 us
    ppermute x3, waiting for transfers between devices, local(): lax.ppermute(plane, 'zh', perm)  2.73 us
  transfers between devices with their start and end apart: 12, of which 7 were waited for; matrix products, arithmetic and copies ran while one was open for 1% of the time, Pallas kernels for 0%

profile of v4, /device:TPU:2, one launch (start us, length us, event | category | flops | bytes accessed | tf_op | source)
XLA Modules:
  0.0 124.0 jit_solution(6831298812473128696)
XLA Ops:
  0.0 0.0 copy-start.4
  0.0 0.0 copy-start.5
  0.0 0.0 copy-start.6
  0.0 1.4 %fusion = s32[]{:T(128)} fusion(s32[4]{0:T(128)} %param.15, s32[4]{0:T(128)} %param.14, s32[]{:T(128)S(6)} %add.57), kind=kLoop, calls=%fused_computation.7 | loop fusion | flops 11 | bytes 40 | tf_op jit(solution)/shard_map/reduce_sum | solution.py:224
  2.0 0.9 dynamic-slice_bitcast_fusion.3
  3.0 7.3 %collective-permute-start.1 = (f32[2,128,128]{2,1,0:T(8,128)S(1)}, f32[2,128,128]{2,1,0:T(8,128)S(1)}, u32[]{:S(2)}, u32[]{:S(2)}) collective-permute-start(f32[2,128,128]{2,1,0:T(8,128)S(1)} %dynamic-slice_bitcast_fusion.3), channel_id=1, source_target_pairs={{0,32},{16,48},{32,0},{48,16},{1,33},{17,49},{33,1},{49,17},{2,34}... | collective-permute-start | bytes 393224 | tf_op jit(solution)/shard_map/ppermute | solution.py:241
  10.2 1.1 dynamic-slice_bitcast_fusion.2
  11.3 1.6 %collective-permute-start.2 = (f32[2,128,128]{2,1,0:T(8,128)S(1)}, f32[2,128,128]{2,1,0:T(8,128)S(1)}, u32[]{:S(2)}, u32[]{:S(2)}) collective-permute-start(f32[2,128,128]{2,1,0:T(8,128)S(1)} %get-tuple-element.28), channel_id=1, source_target_pairs={{0,16},{16,32},{32,48},{48,0},{1,17},{17,33},{33,49},{49,1},{2,18}... | collective-permute-start | bytes 393224 | tf_op jit(solution)/shard_map/ppermute | solution.py:242
  12.9 2.7 %collective-permute-start = (f32[2,128,128]{2,1,0:T(8,128)S(1)}, f32[2,128,128]{2,1,0:T(8,128)S(1)}, u32[]{:S(2)}, u32[]{:S(2)}) collective-permute-start(f32[2,128,128]{2,1,0:T(8,128)S(1)} %get-tuple-element.29), channel_id=1, source_target_pairs={{0,48},{16,0},{32,16},{48,32},{1,49},{17,1},{33,17},{49,33},{2,50}... | collective-permute-start | bytes 393224 | tf_op jit(solution)/shard_map/ppermute | solution.py:240
  15.5 0.0 collective-permute-done.1
  15.6 4.7 %collective-permute-done.2 = f32[2,128,128]{2,1,0:T(8,128)S(1)} collective-permute-done((f32[2,128,128]{2,1,0:T(8,128)S(1)}, f32[2,128,128]{2,1,0:T(8,128)S(1)}, u32[]{:S(2)}, u32[]{:S(2)}) %collective-permute-start.2) | collective-permute-done | bytes 131104 | tf_op jit(solution)/shard_map/ppermute | solution.py:242
  20.3 2.5 %collective-permute-done = f32[2,128,128]{2,1,0:T(8,128)S(1)} collective-permute-done((f32[2,128,128]{2,1,0:T(8,128)S(1)}, f32[2,128,128]{2,1,0:T(8,128)S(1)}, u32[]{:S(2)}, u32[]{:S(2)}) %collective-permute-start) | collective-permute-done | bytes 131104 | tf_op jit(solution)/shard_map/ppermute | solution.py:240
  22.8 1.7 %collective-permute-start.3 = (f32[4,2,128,128]{3,2,1,0:T(8,128)S(1)}, f32[4,2,128,128]{3,2,1,0:T(8,128)S(1)}, u32[]{:S(2)}, u32[]{:S(2)}) collective-permute-start(f32[4,2,128,128]{3,2,1,0:T(8,128)S(1)} %pad_maximum_fusion.refs_4_.own), channel_id=1, source_target_pairs={{0,128},{128,0},{1,129},{129,1},{2,130},{130,2},{3,131},{131,3},{4... | collective-permute-start | bytes 1572872 | tf_op jit(solution)/shard_map/ppermute | solution.py:205
  24.5 0.0 copy-done.6
  24.5 1.4 %collective-permute-start.6 = (f32[1,128,128]{2,1,0:T(8,128)S(1)}, f32[1,128,128]{2,1,0:T(8,128)S(1)}, u32[]{:S(2)}, u32[]{:S(2)}) collective-permute-start(f32[1,128,128]{2,1,0:T(8,128)S(1)} %bitcast.14), channel_id=1, source_target_pairs={{0,16},{16,32},{32,48},{48,0},{1,17},{17,33},{33,49},{49,1},{2,18}... | collective-permute-start | bytes 196616 | tf_op jit(solution)/shard_map/ppermute | solution.py:247
  25.9 4.5 %collective-permute-start.5 = (f32[1,128,128]{2,1,0:T(8,128)S(1)}, f32[1,128,128]{2,1,0:T(8,128)S(1)}, u32[]{:S(2)}, u32[]{:S(2)}) collective-permute-start(f32[1,128,128]{2,1,0:T(8,128)S(1)} %bitcast.15), channel_id=1, source_target_pairs={{0,32},{16,48},{32,0},{48,16},{1,33},{17,49},{33,1},{49,17},{2,34}... | collective-permute-start | bytes 196616 | tf_op jit(solution)/shard_map/ppermute | solution.py:247
  30.4 1.1 collective-permute-start.4
  31.5 0.0 collective-permute-start.7
  31.5 0.0 collective-permute-done.6.refs_3_
  31.6 4.5 %collective-permute-done.5.refs_2_ = f32[1,128,128]{2,1,0:T(8,128)S(1)} collective-permute-done((f32[1,128,128]{2,1,0:T(8,128)S(1)}, f32[1,128,128]{2,1,0:T(8,128)S(1)}, u32[]{:S(2)}, u32[]{:S(2)}) %collective-permute-start.5) | collective-permute-done | bytes 65568 | tf_op jit(solution)/shard_map/ppermute | solution.py:247
  36.1 1.2 %collective-permute-done.4.refs_1_ = f32[1,128,128]{2,1,0:T(8,128)S(1)} collective-permute-done((f32[1,128,128]{2,1,0:T(8,128)S(1)}, f32[1,128,128]{2,1,0:T(8,128)S(1)}, u32[]{:S(2)}, u32[]{:S(2)}) %collective-permute-start.4) | collective-permute-done | bytes 65568 | tf_op jit(solution)/shard_map/ppermute | solution.py:247
  37.3 0.0 collective-permute-done.3.refs_6_.third
  37.3 0.0 collective-permute-start.8
  37.3 0.0 collective-permute-done.7.refs_5_.second
  37.3 1.9 %collective-permute-done.8.refs_7_.fourth = f32[4,2,128,128]{3,2,1,0:T(8,128)S(1)} collective-permute-done((f32[4,2,128,128]{3,2,1,0:T(8,128)S(1)}, f32[4,2,128,128]{3,2,1,0:T(8,128)S(1)}, u32[]{:S(2)}, u32[]{:S(2)}) %collective-permute-start.8) | collective-permute-done | bytes 524320 | tf_op jit(solution)/shard_map/ppermute | solution.py:205
  39.2 0.0 copy-done.4
  39.2 0.0 copy-done.5
  39.2 1.4 %forward_planes.1 = f32[16,32,8,128]{3,2,1,0:T(8,128)S(1)} custom-call(f32[1,128,128]{2,1,0:T(8,128)S(1)} %bitcast.17, f32[1,128,128]{2,1,0:T(8,128)S(1)} %collective-permute-done.4.refs_1_, f32[1,128,128]{2,1,0:T(8,128)S(1)} %collective-permute-done.5.refs_2_, f32[1,128,128]{2,1,0:T(8,128)S(1)} %collective-permute-done.6.refs_3_, ...), custom_call_target="tpu_custom_call" | custom-call | flops 805306368 | bytes 4194304 | tf_op jit(solution)/shard_map/forward_planes/pallas_call | solution.py:165
  40.7 0.0 copy-start.2
  40.7 0.0 copy-start.3
  40.7 0.0 copy-start.7
  40.7 0.0 copy-start.8
  40.7 34.1 %all_to_all.10.spectrum = f32[16,32,8,128]{3,2,1,0:T(8,128)S(1)} all-to-all(f32[16,32,8,128]{3,2,1,0:T(8,128)S(1)} %forward_planes.1), channel_id=1, replica_groups=mesh['yl'=2,'c'=2,'zh'=4,'z0'=2,'x'=4,'yh'=2] {'x','yh','z0'}, dimensions={0} | all-to-all | bytes 4194304 | tf_op jit(solution)/shard_map/all_to_all | solution.py:201
  74.8 0.0 copy-done.2
  74.8 0.0 copy-done.3
  74.8 0.0 copy-done.7
  74.8 0.0 copy-done.8
  74.9 3.2 %solve_columns.1 = f32[16,32,8,128]{3,2,1,0:T(8,128)S(1)} custom-call(f32[16,32,8,128]{3,2,1,0:T(8,128)S(1)} %all_to_all.10.spectrum, f32[64,128]{1,0:T(8,128)S(1)} %copy-done.7, f32[1,128]{1,0:T(1,128)S(1)} %copy-done.8, bf16[256,256]{1,0:T(8,128)(2,1)S(1)} %copy-done.3, bf16[256,256]{1,0:T(8,128)(2,1)S(1)} %copy-done.2), custom_call_target="tpu_custom_call" | custom-call | flops 805306368 | bytes 4194304 | tf_op jit(solution)/shard_map/solve_columns/pallas_call | solution.py:189
  78.1 0.0 copy-start
  78.1 0.0 copy-start.1
  78.1 31.7 %all_to_all.11.potential = f32[16,32,8,128]{3,2,1,0:T(8,128)S(1)} all-to-all(f32[16,32,8,128]{3,2,1,0:T(8,128)S(1)} %solve_columns.1), channel_id=1, replica_groups=mesh['yl'=2,'c'=2,'zh'=4,'z0'=2,'x'=4,'yh'=2] {'x','yh','z0'}, dimensions={0} | all-to-all | bytes 4194304 | tf_op jit(solution)/shard_map/all_to_all | solution.py:201
  109.8 0.0 copy-done
  109.8 0.0 copy-done.1
  109.8 1.1 inverse_planes.3
  111.0 3.0 %collective-permute-start.9 = (f32[128,128]{1,0:T(8,128)S(1)}, f32[128,128]{1,0:T(8,128)S(1)}, u32[]{:S(2)}, u32[]{:S(2)}) collective-permute-start(f32[128,128]{1,0:T(8,128)S(1)} %get-tuple-element.24), channel_id=1, source_target_pairs={{0,16},{16,32},{32,48},{48,0},{1,17},{17,33},{33,49},{49,1},{2,18}... | collective-permute-start | bytes 196616 | tf_op jit(solution)/shard_map/ppermute | solution.py:256
  113.9 3.3 %collective-permute-start.10 = (f32[128,128]{1,0:T(8,128)S(1)}, f32[128,128]{1,0:T(8,128)S(1)}, u32[]{:S(2)}, u32[]{:S(2)}) collective-permute-start(f32[128,128]{1,0:T(8,128)S(1)} %get-tuple-element.25), channel_id=1, source_target_pairs={{0,32},{16,48},{32,0},{48,16},{1,33},{17,49},{33,1},{49,17},{2,34}... | collective-permute-start | bytes 196616 | tf_op jit(solution)/shard_map/ppermute | solution.py:256
  117.3 2.7 %collective-permute-start.11 = (f32[128,128]{1,0:T(8,128)S(1)}, f32[128,128]{1,0:T(8,128)S(1)}, u32[]{:S(2)}, u32[]{:S(2)}) collective-permute-start(f32[128,128]{1,0:T(8,128)S(1)} %get-tuple-element.26), channel_id=1, source_target_pairs={{0,48},{16,0},{32,16},{48,32},{1,49},{17,1},{33,17},{49,33},{2,50}... | collective-permute-start | bytes 196616 | tf_op jit(solution)/shard_map/ppermute | solution.py:256
  120.0 0.6 inverse_planes.2
  120.6 0.0 collective-permute-done.9
  120.6 2.5 %collective-permute-done.10 = f32[128,128]{1,0:T(8,128)S(1)} collective-permute-done((f32[128,128]{1,0:T(8,128)S(1)}, f32[128,128]{1,0:T(8,128)S(1)}, u32[]{:S(2)}, u32[]{:S(2)}) %collective-permute-start.10) | collective-permute-done | bytes 65568 | tf_op jit(solution)/shard_map/ppermute | solution.py:256
  123.1 0.2 collective-permute-done.11
  123.3 0.6 add_bitcast_fusion
  (1 shorter events, 0.0 us)
Async XLA Ops:
  0.0 39.2 %copy-start.4 = (bf16[256,256]{1,0:T(8,128)(2,1)S(1)}, bf16[256,256]{1,0:T(8,128)(2,1)}, u32[]{:S(2)}) copy-start(bf16[256,256]{1,0:T(8,128)(2,1)} %constant.65.clone.refs_9_) | copy-start | bytes 393220
  0.0 39.2 %copy-start.5 = (bf16[256,256]{1,0:T(8,128)(2,1)S(1)}, bf16[256,256]{1,0:T(8,128)(2,1)}, u32[]{:S(2)}) copy-start(bf16[256,256]{1,0:T(8,128)(2,1)} %constant.64.clone.refs_8_) | copy-start | bytes 393220
  0.0 24.5 %copy-start.6 = (f32[1,1,128,128]{3,2,1,0:T(8,128)S(1)}, f32[1,1,128,128]{3,2,1,0:T(8,128)}, u32[]{:S(2)}) copy-start(f32[1,1,128,128]{3,2,1,0:T(8,128)} %param.13) | copy-start | bytes 196612
  3.0 12.6 %collective-permute-start.1 = (f32[2,128,128]{2,1,0:T(8,128)S(1)}, f32[2,128,128]{2,1,0:T(8,128)S(1)}, u32[]{:S(2)}, u32[]{:S(2)}) collective-permute-start(f32[2,128,128]{2,1,0:T(8,128)S(1)} %dynamic-slice_bitcast_fusion.3), channel_id=1, source_target_pairs={{0,32},{16,48},{32,0},{48,16},{1,33},{17,49},{33,1},{49,17},{2,34}... | collective-permute-start | bytes 393224 | tf_op jit(solution)/shard_map/ppermute | solution.py:241
  11.3 9.0 %collective-permute-start.2 = (f32[2,128,128]{2,1,0:T(8,128)S(1)}, f32[2,128,128]{2,1,0:T(8,128)S(1)}, u32[]{:S(2)}, u32[]{:S(2)}) collective-permute-start(f32[2,128,128]{2,1,0:T(8,128)S(1)} %get-tuple-element.28), channel_id=1, source_target_pairs={{0,16},{16,32},{32,48},{48,0},{1,17},{17,33},{33,49},{49,1},{2,18}... | collective-permute-start | bytes 393224 | tf_op jit(solution)/shard_map/ppermute | solution.py:242
  12.9 9.9 %collective-permute-start = (f32[2,128,128]{2,1,0:T(8,128)S(1)}, f32[2,128,128]{2,1,0:T(8,128)S(1)}, u32[]{:S(2)}, u32[]{:S(2)}) collective-permute-start(f32[2,128,128]{2,1,0:T(8,128)S(1)} %get-tuple-element.29), channel_id=1, source_target_pairs={{0,48},{16,0},{32,16},{48,32},{1,49},{17,1},{33,17},{49,33},{2,50}... | collective-permute-start | bytes 393224 | tf_op jit(solution)/shard_map/ppermute | solution.py:240
  22.8 14.5 %collective-permute-start.3 = (f32[4,2,128,128]{3,2,1,0:T(8,128)S(1)}, f32[4,2,128,128]{3,2,1,0:T(8,128)S(1)}, u32[]{:S(2)}, u32[]{:S(2)}) collective-permute-start(f32[4,2,128,128]{3,2,1,0:T(8,128)S(1)} %pad_maximum_fusion.refs_4_.own), channel_id=1, source_target_pairs={{0,128},{128,0},{1,129},{129,1},{2,130},{130,2},{3,131},{131,3},{4... | collective-permute-start | bytes 1572872 | tf_op jit(solution)/shard_map/ppermute | solution.py:205
  24.5 7.1 %collective-permute-start.6 = (f32[1,128,128]{2,1,0:T(8,128)S(1)}, f32[1,128,128]{2,1,0:T(8,128)S(1)}, u32[]{:S(2)}, u32[]{:S(2)}) collective-permute-start(f32[1,128,128]{2,1,0:T(8,128)S(1)} %bitcast.14), channel_id=1, source_target_pairs={{0,16},{16,32},{32,48},{48,0},{1,17},{17,33},{33,49},{49,1},{2,18}... | collective-permute-start | bytes 196616 | tf_op jit(solution)/shard_map/ppermute | solution.py:247
  25.9 10.2 %collective-permute-start.5 = (f32[1,128,128]{2,1,0:T(8,128)S(1)}, f32[1,128,128]{2,1,0:T(8,128)S(1)}, u32[]{:S(2)}, u32[]{:S(2)}) collective-permute-start(f32[1,128,128]{2,1,0:T(8,128)S(1)} %bitcast.15), channel_id=1, source_target_pairs={{0,32},{16,48},{32,0},{48,16},{1,33},{17,49},{33,1},{49,17},{2,34}... | collective-permute-start | bytes 196616 | tf_op jit(solution)/shard_map/ppermute | solution.py:247
  30.4 6.9 %collective-permute-start.4 = (f32[1,128,128]{2,1,0:T(8,128)S(1)}, f32[1,128,128]{2,1,0:T(8,128)S(1)}, u32[]{:S(2)}, u32[]{:S(2)}) collective-permute-start(f32[1,128,128]{2,1,0:T(8,128)S(1)} %bitcast.16), channel_id=1, source_target_pairs={{0,48},{16,0},{32,16},{48,32},{1,49},{17,1},{33,17},{49,33},{2,50}... | collective-permute-start | bytes 196616 | tf_op jit(solution)/shard_map/ppermute | solution.py:247
  31.5 5.8 %collective-permute-start.7 = (f32[4,2,128,128]{3,2,1,0:T(8,128)S(1)}, f32[4,2,128,128]{3,2,1,0:T(8,128)S(1)}, u32[]{:S(2)}, u32[]{:S(2)}) collective-permute-start(f32[4,2,128,128]{3,2,1,0:T(8,128)S(1)} %pad_maximum_fusion.refs_4_.own), channel_id=1, source_target_pairs={{0,64},{64,0},{1,65},{65,1},{2,66},{66,2},{3,67},{67,3},{4,68},{68... | collective-permute-start | bytes 1572872 | tf_op jit(solution)/shard_map/ppermute | solution.py:205
  37.3 1.9 %collective-permute-start.8 = (f32[4,2,128,128]{3,2,1,0:T(8,128)S(1)}, f32[4,2,128,128]{3,2,1,0:T(8,128)S(1)}, u32[]{:S(2)}, u32[]{:S(2)}) collective-permute-start(f32[4,2,128,128]{3,2,1,0:T(8,128)S(1)} %collective-permute-done.3.refs_6_.third), channel_id=1, source_target_pairs={{0,64},{64,0},{1,65},{65,1},{2,66},{66,2},{3,67},{67,3},{4,68},{68... | collective-permute-start | bytes 1572872 | tf_op jit(solution)/shard_map/ppermute | solution.py:205
  40.7 34.2 %copy-start.2 = (bf16[256,256]{1,0:T(8,128)(2,1)S(1)}, bf16[256,256]{1,0:T(8,128)(2,1)}, u32[]{:S(2)}) copy-start(bf16[256,256]{1,0:T(8,128)(2,1)} %constant.69.clone.back) | copy-start | bytes 393220
  40.7 34.2 %copy-start.3 = (bf16[256,256]{1,0:T(8,128)(2,1)S(1)}, bf16[256,256]{1,0:T(8,128)(2,1)}, u32[]{:S(2)}) copy-start(bf16[256,256]{1,0:T(8,128)(2,1)} %constant.68.clone.ahead) | copy-start | bytes 393220
  40.7 34.1 %copy-start.7 = (f32[64,128]{1,0:T(8,128)S(1)}, f32[64,128]{1,0:T(8,128)}, u32[]{:S(2)}) copy-start(f32[64,128]{1,0:T(8,128)} %constant.70.clone.squares) | copy-start | bytes 98308
  40.7 34.1 %copy-start.8 = (f32[1,128]{1,0:T(1,128)S(1)}, f32[1,128]{1,0:T(1,128)}, u32[]{:S(2)}) copy-start(f32[1,128]{1,0:T(1,128)} %constant.71.clone.lanes) | copy-start | bytes 1540
  78.1 31.8 %copy-start = (bf16[256,256]{1,0:T(8,128)(2,1)S(1)}, bf16[256,256]{1,0:T(8,128)(2,1)}, u32[]{:S(2)}) copy-start(bf16[256,256]{1,0:T(8,128)(2,1)} %constant.67.clone.left) | copy-start | bytes 393220
  78.1 31.8 %copy-start.1 = (bf16[256,256]{1,0:T(8,128)(2,1)S(1)}, bf16[256,256]{1,0:T(8,128)(2,1)}, u32[]{:S(2)}) copy-start(bf16[256,256]{1,0:T(8,128)(2,1)} %constant.66.clone.right) | copy-start | bytes 393220
  111.0 9.6 %collective-permute-start.9 = (f32[128,128]{1,0:T(8,128)S(1)}, f32[128,128]{1,0:T(8,128)S(1)}, u32[]{:S(2)}, u32[]{:S(2)}) collective-permute-start(f32[128,128]{1,0:T(8,128)S(1)} %get-tuple-element.24), channel_id=1, source_target_pairs={{0,16},{16,32},{32,48},{48,0},{1,17},{17,33},{33,49},{49,1},{2,18}... | collective-permute-start | bytes 196616 | tf_op jit(solution)/shard_map/ppermute | solution.py:256
  113.9 9.2 %collective-permute-start.10 = (f32[128,128]{1,0:T(8,128)S(1)}, f32[128,128]{1,0:T(8,128)S(1)}, u32[]{:S(2)}, u32[]{:S(2)}) collective-permute-start(f32[128,128]{1,0:T(8,128)S(1)} %get-tuple-element.25), channel_id=1, source_target_pairs={{0,32},{16,48},{32,0},{48,16},{1,33},{17,49},{33,1},{49,17},{2,34}... | collective-permute-start | bytes 196616 | tf_op jit(solution)/shard_map/ppermute | solution.py:256
  117.3 6.0 %collective-permute-start.11 = (f32[128,128]{1,0:T(8,128)S(1)}, f32[128,128]{1,0:T(8,128)S(1)}, u32[]{:S(2)}, u32[]{:S(2)}) collective-permute-start(f32[128,128]{1,0:T(8,128)S(1)} %get-tuple-element.26), channel_id=1, source_target_pairs={{0,48},{16,0},{32,16},{48,32},{1,49},{17,1},{33,17},{49,33},{2,50}... | collective-permute-start | bytes 196616 | tf_op jit(solution)/shard_map/ppermute | solution.py:256
